TPU v7x, 32 devices: a whole 2x2x4 slice. The times are simulated.
32 devices in a mesh: dom: 8 (over z, y), sub: 4 (over x, core).
Axes of the slice: x: 2, y: 2, z: 4, core: 2. Of those that a mesh axis runs over, the one named last changes fastest.
Arguments:
- node_state: bfloat16 [64, 32768], P(None, ('dom', 'sub')), may hold values from -6 to 6
- edge_state: bfloat16 [64, 98304], P(None, ('dom', 'sub')), may hold values from -6 to 6
- senders: int32 [98304], P(('dom', 'sub')), may hold values from 0 to 2559, as said below
- receivers: int32 [98304], P(('dom', 'sub')), may hold values from 0 to 1023
- send_index: int32 [32, 12, 128], P(('dom', 'sub')), may hold values from -1 to 1023, as said below
- node_cotangent: bfloat16 [64, 32768], P(None, ('dom', 'sub')), may hold values from -6 to 6
- edge_cotangent: bfloat16 [64, 98304], P(None, ('dom', 'sub')), may hold values from -6 to 6
- edge_first: bfloat16 [192, 64], replicated, may hold values from -0.4375 to 0.4375
- edge_bias: float32 [64], replicated, may hold values from -3 to 3
- edge_second: bfloat16 [64, 64], replicated, may hold values from -0.75 to 0.75
- edge_gain: float32 [64], replicated, may hold values from 0.1 to 1.9
- edge_shift: float32 [64], replicated, may hold values from -3 to 3
- node_first: bfloat16 [128, 64], replicated, may hold values from -0.5 to 0.5
- node_bias: float32 [64], replicated, may hold values from -3 to 3
- node_second: bfloat16 [64, 64], replicated, may hold values from -0.75 to 0.75
- node_gain: float32 [64], replicated, may hold values from 0.1 to 1.9
Outputs:
- delta_state: bfloat16 [64, 32768], P(None, ('dom', 'sub'))
- delta_edges: bfloat16 [64, 98304], P(None, ('dom', 'sub'))
- delta_edgefirst: float32 [192, 64], replicated
- delta_edgebias: float32 [64], replicated
- delta_edgesecond: float32 [64, 64], replicated
- delta_edgegain: float32 [64], replicated
- delta_edgeshift: float32 [64], replicated
- delta_nodefirst: float32 [128, 64], replicated
- delta_nodebias: float32 [64], replicated
- delta_nodesecond: float32 [64, 64], replicated
- delta_nodegain: float32 [64], replicated
- delta_nodeshift: float32 [64], replicated
Inputs may be any that keep to these rules, and one draw needn't show every extreme that they name: `send_index`: block k = o * 4 + t of partition p = d * 4 + s lists own cells that p sends to the partition at dom index d + o - 1 and sub index t: live entries first, then -1. Blocks towards a dom index outside the mesh, and block 4 + s, hold only -1; every other block holds 32 to 128 live entries. Some partition receives a full block from every partition that sends to it. `senders`: an entry below 1024 is an own cell. An entry 1024 + k * 128 + j with k = o * 4 + u names ghost slot j of block k: the j-th entry of block o * 4 + s of the partition at dom index d + 1 - o and sub index u, and that entry is live.
All inputs are finite; a program needn't handle non-finite values.
Results may differ from a plain program's by a relative error of at most 0.0095.
Values may be sent and summed in bfloat16 or wider, within the bound.
No kernel may reach another device: no remote copies, remote signals or barrier semaphores. Data moves between devices by JAX's collectives and lax.ppermute only.
A program may use at most 64 MiB of HBM per device.

v0:
```python
import math

import jax
import jax.numpy as jnp
from jax import lax
from jax.sharding import PartitionSpec as P

EPSILON = 1e-05


def from_behind(value, axis, steps):
    count = lax.axis_size(axis)
    first, last = (max(0, -steps), min(count, count - steps))
    return lax.ppermute(value, axis, [(source, source + steps) for source in range(first, last)])


def contract_first(first_operand, second_operand):
    return lax.dot_general(
        first_operand, second_operand, (((0,), (0,)), ((), ())), preferred_element_type=jnp.float32
    )


def contract_last(first_operand, second_operand):
    return lax.dot_general(
        first_operand, second_operand, (((1,), (1,)), ((), ())), preferred_element_type=jnp.float32
    )


def sigmoid_linear(values):
    return values * jax.nn.sigmoid(values)


def sigmoid_slope(values):
    logistic = jax.nn.sigmoid(values)
    return logistic * (1.0 + values * (1.0 - logistic))


def standardize(values):
    centered = values - jnp.mean(values, axis=0, keepdims=True)
    spread = lax.rsqrt(jnp.mean(centered * centered, axis=0, keepdims=True) + EPSILON)
    return (centered * spread, spread)


def normalize_back(upstream, scaled, spread, gain_vector):
    gain_delta = jnp.sum(upstream * scaled, axis=1)
    shift_delta = jnp.sum(upstream, axis=1)
    weighted = upstream * gain_vector[:, None]
    result = spread * (
        weighted
        - jnp.mean(weighted, axis=0, keepdims=True)
        - scaled * jnp.mean(weighted * scaled, axis=0, keepdims=True)
    )
    return (result, gain_delta, shift_delta)


def block_sizes(count, width):
    step = math.gcd(count, 512)
    piece = math.gcd(width, 2048)
    return (step, piece)


def pick_precision(values):
    if values.dtype == jnp.float32:
        return lax.Precision.HIGHEST
    return None


def column_gather(table, index):
    rows, width = table.shape
    count = index.shape[0]
    step, piece = block_sizes(count, width)
    blocks = index.reshape(count // step, step)
    precision = pick_precision(table)

    def one_block(number, result):
        chosen = lax.dynamic_index_in_dim(blocks, number, 0, keepdims=False)
        total = jnp.zeros((rows, step), jnp.float32)
        for begin in range(0, width, piece):
            columns = lax.iota(jnp.int32, piece) + begin
            selector = (columns[:, None] == chosen[None, :]).astype(table.dtype)
            total = total + jnp.dot(
                table[:, begin : begin + piece],
                selector,
                precision=precision,
                preferred_element_type=jnp.float32,
            )
        return lax.dynamic_update_slice_in_dim(result, total.astype(table.dtype), number * step, 1)

    return lax.fori_loop(0, count // step, one_block, jnp.zeros((rows, count), table.dtype))


def column_scatter(values, index, width):
    rows, count = values.shape
    step, piece = block_sizes(count, width)
    blocks = index.reshape(count // step, step)
    precision = pick_precision(values)

    def one_block(number, result):
        chosen = lax.dynamic_index_in_dim(blocks, number, 0, keepdims=False)
        portion = lax.dynamic_slice_in_dim(values, number * step, step, 1)
        pieces = []
        for begin in range(0, width, piece):
            columns = lax.iota(jnp.int32, piece) + begin
            selector = (chosen[:, None] == columns[None, :]).astype(values.dtype)
            pieces.append(
                jnp.dot(portion, selector, precision=precision, preferred_element_type=jnp.float32)
            )
        return result + jnp.concatenate(pieces, axis=1)

    return lax.fori_loop(0, count // step, one_block, jnp.zeros((rows, width), jnp.float32))


def local_backward(
    extended,
    node_state,
    edge_state,
    senders,
    receivers,
    node_cotangent,
    edge_cotangent,
    edge_first,
    edge_bias,
    edge_second,
    edge_gain,
    edge_shift,
    node_first,
    node_bias,
    node_second,
    node_gain,
):
    features, cell_count = node_state.shape
    sender_rows = column_gather(extended, senders)
    receiver_rows = column_gather(node_state, receivers)
    stacked = jnp.concatenate([sender_rows, receiver_rows, edge_state], axis=0)
    edge_linear = contract_first(edge_first, stacked) + edge_bias[:, None]
    edge_active = sigmoid_linear(edge_linear).astype(jnp.bfloat16)
    edge_output = contract_first(edge_second, edge_active)
    edge_scaled, edge_spread = standardize(edge_output)
    message = (edge_scaled * edge_gain[:, None] + edge_shift[:, None]).astype(jnp.bfloat16)
    summed = column_scatter(message, receivers, cell_count)
    node_input = jnp.concatenate([node_state, summed.astype(jnp.bfloat16)], axis=0)
    node_linear = contract_first(node_first, node_input) + node_bias[:, None]
    node_active = sigmoid_linear(node_linear).astype(jnp.bfloat16)
    node_output = contract_first(node_second, node_active)
    node_scaled, node_spread = standardize(node_output)
    upstream = node_cotangent.astype(jnp.float32)
    node_delta, nodegain_delta, nodeshift_delta = normalize_back(
        upstream, node_scaled, node_spread, node_gain
    )
    node_delta = node_delta.astype(jnp.bfloat16)
    nodesecond_delta = contract_last(node_active, node_delta)
    node_hidden = jnp.dot(
        node_second, node_delta, preferred_element_type=jnp.float32
    ) * sigmoid_slope(node_linear)
    nodebias_delta = jnp.sum(node_hidden, axis=1)
    node_hidden = node_hidden.astype(jnp.bfloat16)
    nodefirst_delta = contract_last(node_input, node_hidden)
    node_back = jnp.dot(node_first, node_hidden, preferred_element_type=jnp.float32)
    message_delta = edge_cotangent.astype(jnp.float32) + column_gather(
        node_back[features:], receivers
    )
    edge_delta, edgegain_delta, edgeshift_delta = normalize_back(
        message_delta, edge_scaled, edge_spread, edge_gain
    )
    edge_delta = edge_delta.astype(jnp.bfloat16)
    edgesecond_delta = contract_last(edge_active, edge_delta)
    edge_hidden = jnp.dot(
        edge_second, edge_delta, preferred_element_type=jnp.float32
    ) * sigmoid_slope(edge_linear)
    edgebias_delta = jnp.sum(edge_hidden, axis=1)
    edge_hidden = edge_hidden.astype(jnp.bfloat16)
    edgefirst_delta = contract_last(stacked, edge_hidden)
    edge_back = jnp.dot(edge_first, edge_hidden, preferred_element_type=jnp.float32)
    edge_result = (edge_cotangent.astype(jnp.float32) + edge_back[2 * features :]).astype(
        jnp.bfloat16
    )
    scattered = column_scatter(edge_back[:features], senders, extended.shape[1])
    local_delta = (
        scattered[:, :cell_count]
        + column_scatter(edge_back[features : 2 * features], receivers, cell_count)
        + node_back[:features]
        + upstream
    )
    ghost_delta = scattered[:, cell_count:]
    partials = (
        edgefirst_delta,
        edgebias_delta,
        edgesecond_delta,
        edgegain_delta,
        edgeshift_delta,
        nodefirst_delta,
        nodebias_delta,
        nodesecond_delta,
        nodegain_delta,
        nodeshift_delta,
    )
    return (local_delta, ghost_delta, edge_result, partials)


def on_device(
    node_state,
    edge_state,
    senders,
    receivers,
    send_index,
    node_cotangent,
    edge_cotangent,
    edge_first,
    edge_bias,
    edge_second,
    edge_gain,
    edge_shift,
    node_first,
    node_bias,
    node_second,
    node_gain,
):
    features, cell_count = node_state.shape
    sub_count = lax.axis_size("sub")
    peer_count = 3 * sub_count
    halo_width = send_index.shape[2]
    index_rows = send_index.reshape(peer_count, halo_width)
    live_slots = index_rows >= 0
    safe_index = jnp.where(live_slots, index_rows, 0).reshape(-1)
    picked = column_gather(node_state, safe_index).reshape(features, peer_count, halo_width)
    outgoing = jnp.where(live_slots[None], picked, jnp.zeros_like(picked))
    blocks = outgoing.reshape(features, 3, sub_count, halo_width)
    across = lax.all_to_all(blocks, "sub", split_axis=2, concat_axis=2, tiled=True)
    upper = from_behind(across[:, 0], "dom", -1)
    lower = from_behind(across[:, 2], "dom", 1)
    ghost_rows = jnp.stack([upper, across[:, 1], lower], axis=1).reshape(
        features, peer_count, halo_width
    )
    extended = jnp.concatenate([node_state, ghost_rows.reshape(features, -1)], axis=1)
    local_delta, ghost_delta, edge_result, partials = local_backward(
        extended,
        node_state,
        edge_state,
        senders,
        receivers,
        node_cotangent,
        edge_cotangent,
        edge_first,
        edge_bias,
        edge_second,
        edge_gain,
        edge_shift,
        node_first,
        node_bias,
        node_second,
        node_gain,
    )
    ghost_delta = ghost_delta.reshape(features, peer_count, halo_width)
    grouped = ghost_delta.reshape(features, 3, sub_count, halo_width)
    further = from_behind(grouped[:, 0].astype(jnp.bfloat16), "dom", 1).astype(jnp.float32)
    nearer = from_behind(grouped[:, 2].astype(jnp.bfloat16), "dom", -1).astype(jnp.float32)
    regrouped = jnp.stack([further, grouped[:, 1], nearer], axis=1)
    returned = (
        lax.all_to_all(
            regrouped.astype(jnp.bfloat16), "sub", split_axis=2, concat_axis=2, tiled=True
        )
        .astype(regrouped.dtype)
        .reshape(features, peer_count, halo_width)
    )
    masked = jnp.where(live_slots[None], returned, jnp.zeros_like(returned)).reshape(features, -1)
    local_delta = local_delta + column_scatter(masked, safe_index, cell_count)
    totals = lax.psum(
        (
            partials[0],
            partials[1],
            partials[2],
            partials[3],
            partials[4],
            partials[5],
            partials[6],
            partials[7],
            partials[8],
            partials[9],
        ),
        ("dom", "sub"),
    )
    faces_total = edge_state.shape[1] * lax.axis_size("dom") * sub_count
    factor = 1.0 / math.sqrt(faces_total)
    (
        edgefirst_sum,
        edgebias_sum,
        edgesecond_sum,
        edgegain_sum,
        edgeshift_sum,
        nodefirst_sum,
        nodebias_sum,
        nodesecond_sum,
        nodegain_sum,
        nodeshift_sum,
    ) = totals
    return (
        local_delta.astype(jnp.bfloat16),
        edge_result,
        edgefirst_sum * factor,
        edgebias_sum * factor,
        edgesecond_sum * factor,
        edgegain_sum * factor,
        edgeshift_sum * factor,
        nodefirst_sum * factor,
        nodebias_sum * factor,
        nodesecond_sum * factor,
        nodegain_sum * factor,
        nodeshift_sum * factor,
    )


def solution(mesh):
    in_specs = (
        P(None, ("dom", "sub")),
        P(None, ("dom", "sub")),
        P(("dom", "sub")),
        P(("dom", "sub")),
        P(("dom", "sub"), None, None),
        P(None, ("dom", "sub")),
        P(None, ("dom", "sub")),
        P(),
        P(),
        P(),
        P(),
        P(),
        P(),
        P(),
        P(),
        P(),
    )
    out_specs = (
        P(None, ("dom", "sub")),
        P(None, ("dom", "sub")),
        P(),
        P(),
        P(),
        P(),
        P(),
        P(),
        P(),
        P(),
        P(),
        P(),
    )
    return jax.shard_map(
        on_device, mesh=mesh, in_specs=in_specs, out_specs=out_specs, check_vma=False
    )
```

profile of v0, /device:TPU:0, one launch (start us, length us, event | category | flops | bytes accessed | tf_op | source)
XLA Modules:
  0.0 289.3 jit_solution(8450819076300327334)
XLA Ops:
  8.7 4.2 %while.108 = (s32[]{:T(128)}, bf16[64,1536]{1,0:T(8,128)(2,1)S(1)}, s32[3,512]{1,0:T(4,128)S(1)}, bf16[64,1024]{1,0:T(8,128)(2,1)}, s32[]{:T(128)}, /*index=5*/s32[]{:T(128)}, s32[]{:T(128)}, s32[]{:T(128)}) while((s32[]{:T(128)}, bf16[64,1536]{1,0:T(8,128)(2,1)S(1)}, s32[3,512]{1,0:T(4,128)S(1)}, bf16[64,1024]{1,0:T(8,128)(2,1)}, s32[]{:T(128)}, ...), condition=%wide.region_1.2_spmd, body=%wide.region_0.1_spmd.sunk | while | flops 67665928 | bytes 202891 | solution.py:89
  13.8 4.2 %all-to-all-start = ((bf16[64,3,4,128]{3,0,1,2:T(8,128)(2,1)}), bf16[64,3,4,128]{3,0,1,2:T(8,128)(2,1)S(1)}, u32[]{:S(2)}, u32[]{:S(2)}) async-start(bf16[64,3,4,128]{3,0,1,2:T(8,128)(2,1)} %copy.47), calls=%async_computation | async-start | bytes 393216 | tf_op jit(solution)/shard_map/all_to_all | solution.py:228
  18.1 5.3 %all-to-all-done = bf16[64,3,4,128]{3,0,1,2:T(8,128)(2,1)S(1)} async-done(((bf16[64,3,4,128]{3,0,1,2:T(8,128)(2,1)}), bf16[64,3,4,128]{3,0,1,2:T(8,128)(2,1)S(1)}, u32[]{:S(2)}, u32[]{:S(2)}) %all-to-all-start) | async-done | bytes 196640 | tf_op jit(solution)/shard_map/all_to_all | solution.py:228
  23.4 4.0 %collective-permute-start.1 = (bf16[64,4,128]{2,0,1:T(8,128)(2,1)S(1)}, bf16[64,4,128]{2,0,1:T(8,128)(2,1)S(1)}, u32[]{:S(2)}, u32[]{:S(2)}) collective-permute-start(bf16[64,4,128]{2,0,1:T(8,128)(2,1)S(1)} %get-tuple-element.818), channel_id=1, source_target_pairs={{0,4},{4,8},{8,12},{12,16},{16,20},{20,24},{24,28},{1,5},{5,9},{9,... | collective-permute-start | bytes 196616 | tf_op jit(solution)/shard_map/ppermute | solution.py:14
  28.8 3.0 %while.110 = (s32[]{:T(128)}, bf16[64,3072]{1,0:T(8,128)(2,1)S(1)}, s32[6,512]{1,0:T(8,128)S(1)}, bf16[64,1024]{1,0:T(8,128)(2,1)S(1)}, s32[]{:T(128)}, /*index=5*/s32[]{:T(128)}, s32[]{:T(128)}, s32[]{:T(128)}) while((s32[]{:T(128)}, bf16[64,3072]{1,0:T(8,128)(2,1)S(1)}, s32[6,512]{1,0:T(8,128)S(1)}, bf16[64,1024]{1,0:T(8,128)(2,1)S(1)}, ...), condition=%wide.region_5.6_spmd, body=%wide.region_4.5_spmd.sunk | while | flops 67665928 | bytes 202891 | solution.py:89
  31.9 1.7 collective-permute-done
  33.9 11.0 %while.109 = (s32[]{:T(128)}, bf16[64,3072]{1,0:T(8,128)(2,1)S(1)}, s32[6,512]{1,0:T(8,128)S(1)}, bf16[64,1024]{1,0:T(8,128)(2,1)S(1)}, bf16[64,1536]{1,0:T(8,12...) while((s32[]{:T(128)}, bf16[64,3072]{1,0:T(8,128)(2,1)S(1)}, s32[6,512]{1,0:T(8,128)S(1)}, ...), condition=%wide.region_3.4_spmd, body=%wide.region_2.3_spmd.sunk | while | flops 169248768 | bytes 1472659 | solution.py:89
  48.3 3.7 %while.112 = (s32[]{:T(128)}, f32[64,1024]{1,0:T(8,128)S(1)}, bf16[64,3072]{1,0:T(8,128)(2,1)S(1)}, s32[6,512]{1,0:T(8,128)S(1)}, s32[]{:T(128)}, /*index=5*/s32[]{:T(128)}, s32[]{:T(128)}, s32[]{:T(128)}) while((s32[]{:T(128)}, f32[64,1024]{1,0:T(8,128)S(1)}, bf16[64,3072]{1,0:T(8,128)(2,1)S(1)}, s32[6,512]{1,0:T(8,128)S(1)}, ...), condition=%wide.region_9.10_spmd.clone, body=%wide.region_8.9_spmd.clone.sunk | while | flops 67764232 | bytes 596117 | solution.py:110
  57.2 11.1 %while.111 = (s32[]{:T(128)}, f32[64,3072]{1,0:T(8,128)S(1)}, s32[6,512]{1,0:T(8,128)S(1)}, f32[64,1024]{1,0:T(8,128)}, s32[]{:T(128)}, /*index=5*/s32[]{:T(128)}, s32[]{:T(128)}, s32[]{:T(128)}) while((s32[]{:T(128)}, f32[64,3072]{1,0:T(8,128)S(1)}, s32[6,512]{1,0:T(8,128)S(1)}, f32[64,1024]{1,0:T(8,128)}, s32[]{:T(128)}, ...), condition=%wide.region_15.16_spmd, body=%wide.region_14.15_spmd.sunk | while | flops 403177472 | bytes 399499 | solution.py:89
  57.2 1.8 fusion.184
  59.1 1.8 fusion.184
  60.9 1.8 fusion.184
  62.8 1.8 fusion.184
  64.6 1.8 fusion.184
  66.5 1.8 fusion.184
  75.0 45.6 %while.113 = (s32[]{:T(128)}, f32[64,2560]{1,0:T(8,128)S(1)}, f32[64,3072]{1,0:T(8,128)}, s32[6,512]{1,0:T(8,128)S(1)}, s32[]{:T(128)}, /*index=5*/s32[]{:T(128)}, s32[]{:T(128)}, s32[]{:T(128)}) while((s32[]{:T(128)}, f32[64,2560]{1,0:T(8,128)S(1)}, f32[64,3072]{1,0:T(8,128)}, s32[6,512]{1,0:T(8,128)S(1)}, s32[]{:T(128)}, ...), condition=%wide.region_19.20_spmd.clone, body=%wide.region_18.19_spmd.clone.sunk | while | flops 1008273408 | bytes 3307685 | solution.py:110
  75.0 1.5 convolution_dynamic-update-slice_fusion.10
  97.8 1.5 convolution_dynamic-update-slice_fusion.10
  120.8 4.3 %collective-permute-start.2 = (bf16[64,4,128]{2,1,0:T(4,128)(2,1)S(1)}, bf16[64,4,128]{2,1,0:T(4,128)(2,1)S(1)}, u32[]{:S(2)}, u32[]{:S(2)}) collective-permute-start(bf16[64,4,128]{2,1,0:T(4,128)(2,1)S(1)} %get-tuple-element.814), channel_id=1, source_target_pairs={{0,4},{4,8},{8,12},{12,16},{16,20},{20,24},{24,28},{1,5},{5,9},{9,... | collective-permute-start | bytes 196616 | tf_op jit(solution)/shard_map/ppermute | solution.py:14
  126.6 6.2 %while.114 = (s32[]{:T(128)}, f32[64,1024]{1,0:T(8,128)S(1)}, f32[64,3072]{1,0:T(8,128)S(1)}, s32[6,512]{1,0:T(8,128)S(1)}, s32[]{:T(128)}, /*index=5*/s32[]{:T(128)}, s32[]{:T(128)}, s32[]{:T(128)}) while((s32[]{:T(128)}, f32[64,1024]{1,0:T(8,128)S(1)}, f32[64,3072]{1,0:T(8,128)S(1)}, s32[6,512]{1,0:T(8,128)S(1)}, s32[]{:T(128)}, ...), condition=%wide.region_21.22_spmd.clone, body=%wide.region_20.21_spmd.clone.sunk | while | flops 403308544 | bytes 661653 | solution.py:110
  132.9 124.5 %all-reduce.3.cloned.1.call-done = (f32[192,64]{0,1:T(8,128)}, f32[64]{0:T(128)}, f32[64,64]{1,0:T(8,128)}, f32[64]{0:T(128)}, f32[64]{0:T(128)}, /*index=5*/f32...) async-done(((f32[192,64]{0,1:T(8,128)}, f32[64]{0:T(128)}, f32[64,64]{1,0:T(8,128)}, f32[64]{0:T(128)}, f32[64]{0:T(128)}, ...) | async-done | bytes 116240 | tf_op jit(solution)/shard_map/psum | solution.py:267
  269.6 3.4 %all-to-all-start.1 = ((bf16[64,3,4,128]{3,0,1,2:T(8,128)(2,1)}), bf16[64,3,4,128]{3,0,1,2:T(8,128)(2,1)S(1)}, u32[]{:S(2)}, u32[]{:S(2)}) async-start(bf16[64,3,4,128]{3,0,1,2:T(8,128)(2,1)} %copy.54), calls=%async_computation.1 | async-start | bytes 393216 | tf_op jit(solution)/shard_map/all_to_all | solution.py:259
  274.1 4.1 %all-to-all-done.1 = bf16[64,3,4,128]{3,0,1,2:T(8,128)(2,1)S(1)} async-done(((bf16[64,3,4,128]{3,0,1,2:T(8,128)(2,1)}), bf16[64,3,4,128]{3,0,1,2:T(8,128)(2,1)S(1)}, u32[]{:S(2)}, u32[]{:S(2)}) %all-to-all-start.1) | async-done | bytes 196640 | tf_op jit(solution)/shard_map/all_to_all | solution.py:259
  278.6 3.1 %while.115 = (s32[]{:T(128)}, f32[64,1024]{1,0:T(8,128)S(1)}, f32[64,1536]{1,0:T(8,128)S(1)}, s32[3,512]{1,0:T(4,128)S(1)}, s32[]{:T(128)}, /*index=5*/s32[]{:T(128)}, s32[]{:T(128)}, s32[]{:T(128)}) while((s32[]{:T(128)}, f32[64,1024]{1,0:T(8,128)S(1)}, f32[64,1536]{1,0:T(8,128)S(1)}, s32[3,512]{1,0:T(4,128)S(1)}, s32[]{:T(128)}, ...), condition=%wide.region_23.24_spmd.clone, body=%wide.region_22.23_spmd.clone.sunk | while | flops 403308544 | bytes 661653 | solution.py:110
  (302 shorter events, 107.2 us)
Async XLA Ops:
  7.2 37.9 %copy-start = (bf16[192,64]{0,1:T(8,128)(2,1)S(1)}, bf16[192,64]{0,1:T(8,128)(2,1)}, u32[]{:S(2)}) copy-start(bf16[192,64]{0,1:T(8,128)(2,1)} %param.39) | copy-start | bytes 73732
  8.7 9.4 %copy-start.13 = (s32[3072]{0:T(1024)S(1)}, s32[3072]{0:T(1024)}, u32[]{:S(2)}) copy-start(s32[3072]{0:T(1024)} %param.35) | copy-start | bytes 36868
  12.9 15.8 %copy-start.18 = (bf16[64,1024]{1,0:T(8,128)(2,1)S(1)}, bf16[64,1024]{1,0:T(8,128)(2,1)}, u32[]{:S(2)}) copy-start(bf16[64,1024]{1,0:T(8,128)(2,1)} %get-tuple-element.1290) | copy-start | bytes 393220
  13.8 9.5 %all-to-all-start = ((bf16[64,3,4,128]{3,0,1,2:T(8,128)(2,1)}), bf16[64,3,4,128]{3,0,1,2:T(8,128)(2,1)S(1)}, u32[]{:S(2)}, u32[]{:S(2)}) async-start(bf16[64,3,4,128]{3,0,1,2:T(8,128)(2,1)} %copy.47), calls=%async_computation | async-start | bytes 393216 | tf_op jit(solution)/shard_map/all_to_all | solution.py:228
  18.1 239.3 %all-reduce.3.cloned.1.call-start = ((), (), s32[]{:S(2)}) async-start(), calls=%async_computation.2 | async-start | bytes 333824 | tf_op jit(solution)/shard_map/psum | solution.py:267
  23.4 8.5 %collective-permute-start.1 = (bf16[64,4,128]{2,0,1:T(8,128)(2,1)S(1)}, bf16[64,4,128]{2,0,1:T(8,128)(2,1)S(1)}, u32[]{:S(2)}, u32[]{:S(2)}) collective-permute-start(bf16[64,4,128]{2,0,1:T(8,128)(2,1)S(1)} %get-tuple-element.818), channel_id=1, source_target_pairs={{0,4},{4,8},{8,12},{12,16},{16,20},{20,24},{24,28},{1,5},{5,9},{9,... | collective-permute-start | bytes 196616 | tf_op jit(solution)/shard_map/ppermute | solution.py:14
  27.4 6.2 %collective-permute-start = (bf16[64,4,128]{2,0,1:T(8,128)(2,1)S(1)}, bf16[64,4,128]{2,0,1:T(8,128)(2,1)S(1)}, u32[]{:S(2)}, u32[]{:S(2)}) collective-permute-start(bf16[64,4,128]{2,0,1:T(8,128)(2,1)S(1)} %get-tuple-element.817), channel_id=1, source_target_pairs={{4,0},{8,4},{12,8},{16,12},{20,16},{24,20},{28,24},{5,1},{9,5},{13... | collective-permute-start | bytes 196616 | tf_op jit(solution)/shard_map/ppermute | solution.py:14
  28.8 3.1 %copy-start.14 = (s32[3072]{0:T(1024)S(1)}, s32[3072]{0:T(1024)}, u32[]{:S(2)}) copy-start(s32[3072]{0:T(1024)} %param.34) | copy-start | bytes 36868
  33.9 11.1 %copy-start.7 = (bf16[64,3072]{1,0:T(8,128)(2,1)S(1)}, bf16[64,3072]{1,0:T(8,128)(2,1)}, u32[]{:S(2)}) copy-start(bf16[64,3072]{1,0:T(8,128)(2,1)} %param.33) | copy-start | bytes 1179652
  45.6 1.3 copy-start.2
  45.6 2.0 copy-start.10
  45.6 2.5 copy-start.15
  45.6 2.5 copy-start.17
  48.3 3.8 %copy-start.12 = (bf16[128,64]{0,1:T(8,128)(2,1)S(1)}, bf16[128,64]{0,1:T(8,128)(2,1)}, u32[]{:S(2)}) copy-start(bf16[128,64]{0,1:T(8,128)(2,1)} %param.44) | copy-start | bytes 49156
  48.3 3.8 %copy-start.20 = (f32[64]{0:T(128)S(1)}, f32[64]{0:T(128)}, u32[]{:S(2)}) copy-start(f32[64]{0:T(128)} %param.45) | copy-start | bytes 772
  48.3 4.0 %copy-start.11 = (bf16[64,64]{1,0:T(8,128)(2,1)S(1)}, bf16[64,64]{1,0:T(8,128)(2,1)}, u32[]{:S(2)}) copy-start(bf16[64,64]{1,0:T(8,128)(2,1)} %param.46) | copy-start | bytes 24580
  57.2 11.2 %copy-start.1 = (bf16[64,3072]{1,0:T(8,128)(2,1)S(1)}, bf16[64,3072]{1,0:T(8,128)(2,1)}, u32[]{:S(2)}) copy-start(bf16[64,3072]{1,0:T(8,128)(2,1)} %param.38) | copy-start | bytes 1179652
  68.3 1.7 copy-start.5
  70.9 1.3 copy-start.3
  75.0 51.6 %copy-start.9 = (f32[64,1024]{1,0:T(8,128)S(1)}, f32[64,1024]{1,0:T(8,128)}, u32[]{:S(2)}) copy-start(f32[64,1024]{1,0:T(8,128)} %custom-call.2) | copy-start | bytes 786436
  120.8 147.9 %collective-permute-start.2 = (bf16[64,4,128]{2,1,0:T(4,128)(2,1)S(1)}, bf16[64,4,128]{2,1,0:T(4,128)(2,1)S(1)}, u32[]{:S(2)}, u32[]{:S(2)}) collective-permute-start(bf16[64,4,128]{2,1,0:T(4,128)(2,1)S(1)} %get-tuple-element.814), channel_id=1, source_target_pairs={{0,4},{4,8},{8,12},{12,16},{16,20},{20,24},{24,28},{1,5},{5,9},{9,... | collective-permute-start | bytes 196616 | tf_op jit(solution)/shard_map/ppermute | solution.py:14
  125.1 143.6 %collective-permute-start.3 = (bf16[64,4,128]{2,1,0:T(4,128)(2,1)S(1)}, bf16[64,4,128]{2,1,0:T(4,128)(2,1)S(1)}, u32[]{:S(2)}, u32[]{:S(2)}) collective-permute-start(bf16[64,4,128]{2,1,0:T(4,128)(2,1)S(1)} %get-tuple-element.815), channel_id=1, source_target_pairs={{4,0},{8,4},{12,8},{16,12},{20,16},{24,20},{28,24},{5,1},{9,5},{13... | collective-permute-start | bytes 196616 | tf_op jit(solution)/shard_map/ppermute | solution.py:14
  132.8 145.7 %copy-start.8 = (f32[64,1024]{1,0:T(8,128)S(1)}, f32[64,1024]{1,0:T(8,128)}, u32[]{:S(2)}) copy-start(f32[64,1024]{1,0:T(8,128)} %custom-call.3) | copy-start | bytes 786436
  269.6 8.6 %all-to-all-start.1 = ((bf16[64,3,4,128]{3,0,1,2:T(8,128)(2,1)}), bf16[64,3,4,128]{3,0,1,2:T(8,128)(2,1)S(1)}, u32[]{:S(2)}, u32[]{:S(2)}) async-start(bf16[64,3,4,128]{3,0,1,2:T(8,128)(2,1)} %copy.54), calls=%async_computation.1 | async-start | bytes 393216 | tf_op jit(solution)/shard_map/all_to_all | solution.py:259
  (5 other events, 4.4 us)
Sparse Core Ops, SparseCore 0:
  126.7 130.6 all-reduce.2
where the time goes:
time: 291 us; the launch traced here: 289 us
  waiting for transfers between devices  136 us (47%)
  matrix products  92.7 us (32%)
  other arithmetic  20.3 us (7%)
  starting transfers between devices  18.7 us (6%)
  between operations  14.6 us (5%)
  local copies, waits for them, and re-layouts  5.33 us (2%)
    psum x1, waiting for transfers between devices, on_device(): lax.psum((partials[0], partials[1], partials[2], partials[3], partials[4]...  125 us
    dot_general x45, matrix products, one_block(): jnp.dot(portion, selector, precision=precision, preferred_element_type=jn...  56.2 us
    dot_general x45, matrix products, one_block(): jnp.dot(table[:, begin:begin + piece], selector, precision=precision, pre...  28.1 us
    ppermute x4, starting transfers between devices, from_behind(): lax.ppermute(value, axis, [(source, source + steps) for source in range(f...  11.1 us
  transfers between devices with their start and end apart: 7, of which 4 were waited for; matrix products, arithmetic and copies ran while one was open for 7% of the time, Pallas kernels for 0%

commit v1 on v0

v1 whole, which is shorter than its diff:
```python
import functools
import math

import jax
import jax.numpy as jnp
from jax import lax
from jax.experimental import pallas as pl
from jax.experimental.pallas import tpu as pltpu
from jax.sharding import PartitionSpec as P

EPSILON = 1e-05
LOW = 256
F32 = jnp.float32
BF16 = jnp.bfloat16
VECTORS = 6


def mm(a, b):
    return lax.dot_general(a, b, (((1,), (0,)), ((), ())), preferred_element_type=F32)


def mm_nt(a, b):
    return lax.dot_general(a, b, (((1,), (1,)), ((), ())), preferred_element_type=F32)


def low_hot(index):
    rows = lax.broadcasted_iota(jnp.int32, (LOW, index.shape[1]), 0)
    return jnp.where(rows == (index & (LOW - 1)), 1.0, 0.0).astype(BF16)


def pick_high(stack, index, features):
    high = index >> 8
    blocks = stack.shape[0] // features
    result = jnp.zeros((features, stack.shape[1]), stack.dtype)
    for number in range(blocks):
        part = stack[number * features : (number + 1) * features]
        result = jnp.where(high == number, part, result)
    return result


def spread_high(values, index, blocks):
    high = index >> 8
    zero = jnp.zeros_like(values)
    return jnp.concatenate(
        [jnp.where(high == number, values, zero).astype(BF16) for number in range(blocks)], axis=0
    )


def stack_table(table):
    return jnp.concatenate(
        [table[:, begin : begin + LOW] for begin in range(0, table.shape[1], LOW)], axis=0
    )


def unstack(stack, features):
    return jnp.concatenate(
        [stack[begin : begin + features] for begin in range(0, stack.shape[0], features)], axis=1
    )


def sigmoid(values):
    return 1.0 / (1.0 + jnp.exp(-values))


def standardize(values):
    centered = values - jnp.mean(values, axis=0, keepdims=True)
    spread = lax.rsqrt(jnp.mean(centered * centered, axis=0, keepdims=True) + EPSILON)
    return centered * spread, spread


def norm_back(upstream, scaled, spread, gain):
    weighted = upstream * gain
    return spread * (
        weighted
        - jnp.mean(weighted, axis=0, keepdims=True)
        - scaled * jnp.mean(weighted * scaled, axis=0, keepdims=True)
    )


def pair_rows(index_ref, first):
    return jnp.concatenate([index_ref[first : first + 1], index_ref[first + 1 : first + 2]], axis=1)


def pick_kernel(node_ref, index_ref, out_ref):
    features = node_ref.shape[0]
    subs = out_ref.shape[0]
    halo = index_ref.shape[1]
    table = stack_table(node_ref[...])
    for first in range(0, index_ref.shape[0], 2):
        index = pair_rows(index_ref, first)
        chosen = pick_high(mm(table, low_hot(index)), index, features).astype(BF16)
        for extra in range(2):
            block = first + extra
            out_ref[block % subs, block // subs] = chosen[:, extra * halo : (extra + 1) * halo]


def main_kernel(
    node_ref,
    across_ref,
    upper_ref,
    lower_ref,
    edge_ref,
    senders_ref,
    receivers_ref,
    nodecot_ref,
    edgecot_ref,
    edgefirst_ref,
    edgesecond_ref,
    nodefirst_ref,
    nodesecond_ref,
    vectors_ref,
    local_ref,
    ghost_ref,
    result_ref,
    partial_ref,
    table_ref,
    shot_ref,
    rhot_ref,
    slope_ref,
    active_ref,
    scaled_ref,
    spread_ref,
    *,
    tile,
    factor,
):
    features, cells = node_ref.shape
    faces = edge_ref.shape[1]
    subs, halo = upper_ref.shape[0], upper_ref.shape[2]
    own = cells // LOW
    total = table_ref.shape[0] // features
    vectors = vectors_ref[...]
    edge_bias, edge_gain, edge_shift, node_bias, node_gain = [
        vectors[:, number : number + 1] for number in range(5)
    ]
    first_t = edgefirst_ref[...]
    second = edgesecond_ref[...]
    second_t = second.astype(F32).T.astype(BF16)
    first = first_t.astype(F32).T.astype(BF16)

    node_state = node_ref[...]
    table_ref[: own * features] = stack_table(node_state)
    for block in range(3 * subs):
        source = (
            upper_ref[block % subs]
            if block < subs
            else (across_ref[block % subs, 1] if block < 2 * subs else lower_ref[block % subs])
        )
        column = block * halo
        row = (own + column // LOW) * features
        table_ref[row : row + features, column % LOW : column % LOW + halo] = source

    summed = jnp.zeros((own * features, LOW), F32)
    for begin in range(0, faces, tile):
        at = slice(begin, begin + tile)
        sender, receiver = senders_ref[:, at], receivers_ref[:, at]
        shot, rhot = low_hot(sender), low_hot(receiver)
        shot_ref[:, at] = shot
        rhot_ref[:, at] = rhot
        sender_rows = pick_high(mm(table_ref[...], shot), sender, features).astype(BF16)
        receiver_rows = pick_high(
            mm(table_ref[: own * features], rhot), receiver, features
        ).astype(BF16)
        stacked = jnp.concatenate([sender_rows, receiver_rows, edge_ref[:, at]], axis=0)
        linear = mm(first_t, stacked) + edge_bias
        logistic = sigmoid(linear)
        slope_ref[:, at] = logistic * (1.0 + linear * (1.0 - logistic))
        active = (linear * logistic).astype(BF16)
        active_ref[:, at] = active
        scaled, spread = standardize(mm(second_t, active))
        scaled_ref[:, at] = scaled
        spread_ref[:, at] = spread
        message = (scaled * edge_gain + edge_shift).astype(BF16).astype(F32)
        summed = summed + mm_nt(spread_high(message, receiver, own), rhot)

    node_first_t = nodefirst_ref[...]
    node_first = node_first_t.astype(F32).T.astype(BF16)
    node_second = nodesecond_ref[...]
    node_second_t = node_second.astype(F32).T.astype(BF16)
    node_input = jnp.concatenate([node_state, unstack(summed, features).astype(BF16)], axis=0)
    node_linear = mm(node_first_t, node_input) + node_bias
    node_logistic = sigmoid(node_linear)
    node_active = (node_linear * node_logistic).astype(BF16)
    node_scaled, node_spread = standardize(mm(node_second_t, node_active))
    upstream = nodecot_ref[...].astype(F32)
    nodegain_delta = jnp.sum(upstream * node_scaled, axis=1, keepdims=True)
    nodeshift_delta = jnp.sum(upstream, axis=1, keepdims=True)
    node_delta = norm_back(upstream, node_scaled, node_spread, node_gain).astype(BF16)
    nodesecond_delta = mm_nt(node_active, node_delta)
    node_hidden = mm(node_second, node_delta) * (
        node_logistic * (1.0 + node_linear * (1.0 - node_logistic))
    )
    nodebias_delta = jnp.sum(node_hidden, axis=1, keepdims=True)
    node_hidden = node_hidden.astype(BF16)
    nodefirst_delta = mm_nt(node_input, node_hidden)
    node_back = mm(node_first, node_hidden)
    local = upstream + node_back[:features]
    back_table = stack_table(node_back[features:]).astype(BF16)

    sender_sum = jnp.zeros((total * features, LOW), F32)
    receiver_sum = jnp.zeros((own * features, LOW), F32)
    gain_sum = jnp.zeros((features, tile), F32)
    shift_sum = jnp.zeros((features, tile), F32)
    bias_sum = jnp.zeros((features, tile), F32)
    edgesecond_delta = jnp.zeros((features, features), F32)
    edgethird_delta = jnp.zeros((features, features), F32)
    first_s, first_r, first_e = [
        first[number * features : (number + 1) * features] for number in range(3)
    ]
    for begin in range(0, faces, tile):
        at = slice(begin, begin + tile)
        sender, receiver = senders_ref[:, at], receivers_ref[:, at]
        shot, rhot = shot_ref[:, at], rhot_ref[:, at]
        cotangent = edgecot_ref[:, at].astype(F32)
        scaled = scaled_ref[:, at]
        message_delta = cotangent + pick_high(mm(back_table, rhot), receiver, features)
        gain_sum = gain_sum + message_delta * scaled
        shift_sum = shift_sum + message_delta
        delta = norm_back(message_delta, scaled, spread_ref[:, at], edge_gain).astype(BF16)
        edgesecond_delta = edgesecond_delta + mm_nt(active_ref[:, at], delta)
        hidden = mm(second, delta) * slope_ref[:, at]
        bias_sum = bias_sum + hidden
        rounded = hidden.astype(BF16)
        result_ref[:, at] = (cotangent + mm(first_e, rounded)).astype(BF16)
        edgethird_delta = edgethird_delta + mm_nt(edge_ref[:, at], rounded)
        wide = rounded.astype(F32)
        sender_sum = sender_sum + mm_nt(spread_high(wide, sender, total), shot)
        receiver_sum = receiver_sum + mm_nt(spread_high(wide, receiver, own), rhot)

    sender_sum = sender_sum.astype(BF16)
    receiver_sum = unstack(receiver_sum, features).astype(BF16)
    edgefirst_s = jnp.zeros((features, features), F32)
    for number in range(total):
        rows = slice(number * features, (number + 1) * features)
        edgefirst_s = edgefirst_s + mm_nt(table_ref[rows], sender_sum[rows])
    edgefirst_r = mm_nt(node_state, receiver_sum)
    spread_out = mm(first_s, unstack(sender_sum, features))
    local_ref[...] = local + spread_out[:, :cells] + mm(first_r, receiver_sum)
    for block in range(3 * subs):
        column = cells + block * halo
        ghost_ref[block % subs, block // subs] = spread_out[:, column : column + halo].astype(BF16)

    columns = [
        jnp.sum(bias_sum, axis=1, keepdims=True),
        jnp.sum(gain_sum, axis=1, keepdims=True),
        jnp.sum(shift_sum, axis=1, keepdims=True),
        nodebias_delta,
        nodegain_delta,
        nodeshift_delta,
    ]
    lanes = lax.broadcasted_iota(jnp.int32, (features, features), 1)
    vector_block = jnp.zeros((features, features), F32)
    for number, column in enumerate(columns):
        vector_block = jnp.where(lanes == number, column, vector_block)
    pairs = (
        (edgefirst_s, edgefirst_r),
        (edgethird_delta, edgesecond_delta),
        (nodefirst_delta[:features], nodefirst_delta[features:]),
        (nodesecond_delta, vector_block),
    )
    for number, (left, right) in enumerate(pairs):
        partial_ref[number * features : (number + 1) * features] = (
            jnp.concatenate([left, right], axis=1) * factor
        )


def final_kernel(
    local_ref,
    across_ref,
    further_ref,
    nearer_ref,
    index_ref,
    totals_ref,
    state_ref,
    edgefirst_ref,
    edgesecond_ref,
    nodefirst_ref,
    nodesecond_ref,
    vector_ref,
):
    features, cells = local_ref.shape
    subs = further_ref.shape[0]
    own = cells // LOW

    def returned(block):
        group = block // subs
        if group == 0:
            return further_ref[block % subs]
        if group == 1:
            return across_ref[block % subs, 1]
        return nearer_ref[block % subs]

    total = jnp.zeros((own * features, LOW), F32)
    for first in range(0, index_ref.shape[0], 2):
        index = pair_rows(index_ref, first)
        values = jnp.concatenate([returned(first), returned(first + 1)], axis=1).astype(F32)
        total = total + mm_nt(spread_high(values, index, own), low_hot(index))
    state_ref[...] = (local_ref[...] + unstack(total, features)).astype(BF16)

    sums = [totals_ref[number * features : (number + 1) * features] for number in range(4)]
    halves = [(part[:, :features], part[:, features:]) for part in sums]
    edgefirst_ref[...] = jnp.concatenate([halves[0][0], halves[0][1], halves[1][0]], axis=0).T
    edgesecond_ref[...] = halves[1][1]
    nodefirst_ref[...] = jnp.concatenate([halves[2][0], halves[2][1]], axis=0).T
    nodesecond_ref[...] = halves[3][0]
    vector_ref[...] = halves[3][1].T[: vector_ref.shape[0]]


def shift(value, steps):
    count = lax.axis_size("dom")
    first, last = max(0, -steps), min(count, count - steps)
    return lax.ppermute(value, "dom", [(source, source + steps) for source in range(first, last)])


def exchange(blocks):
    across = lax.all_to_all(blocks, "sub", split_axis=0, concat_axis=0, tiled=True)
    return across, across[:, 0], across[:, 2]


def total_over(value):
    for axis in ("sub", "dom"):
        count = lax.axis_size(axis)
        if count & (count - 1):
            value = lax.psum(value, axis)
            continue
        step = 1
        while step < count:
            value = value + lax.ppermute(value, axis, [(i, i ^ step) for i in range(count)])
            step *= 2
    return value


def on_device(
    node_state,
    edge_state,
    senders,
    receivers,
    send_index,
    node_cotangent,
    edge_cotangent,
    edge_first,
    edge_bias,
    edge_second,
    edge_gain,
    edge_shift,
    node_first,
    node_bias,
    node_second,
    node_gain,
):
    features, cells = node_state.shape
    faces = edge_state.shape[1]
    subs = lax.axis_size("sub")
    halo = send_index.shape[2]
    blocks = 3 * subs
    index = send_index.reshape(blocks, halo)
    faces_total = faces * lax.axis_size("dom") * subs
    factor = 1.0 / math.sqrt(faces_total)
    wide = cells + blocks * halo
    tile = math.gcd(faces, 512)
    shape = jax.ShapeDtypeStruct
    ghost_shape = shape((subs, 3, features, halo), BF16)

    outgoing = pl.pallas_call(pick_kernel, out_shape=ghost_shape, name="pick")(node_state, index)
    across, up, down = exchange(outgoing)
    upper, lower = shift(up, -1), shift(down, 1)
    vectors = jnp.stack([edge_bias, edge_gain, edge_shift, node_bias, node_gain], axis=1)
    local, ghost, edge_result, partial = pl.pallas_call(
        functools.partial(main_kernel, tile=tile, factor=factor),
        out_shape=(
            shape((features, cells), F32),
            ghost_shape,
            shape((features, faces), BF16),
            shape((4 * features, 2 * features), F32),
        ),
        scratch_shapes=[
            pltpu.VMEM((wide // LOW * features, LOW), BF16),
            pltpu.VMEM((LOW, faces), BF16),
            pltpu.VMEM((LOW, faces), BF16),
            pltpu.VMEM((features, faces), F32),
            pltpu.VMEM((features, faces), BF16),
            pltpu.VMEM((features, faces), F32),
            pltpu.VMEM((1, faces), F32),
        ],
        compiler_params=pltpu.CompilerParams(vmem_limit_bytes=48 * 1024 * 1024),
        name="main",
    )(
        node_state,
        across,
        upper,
        lower,
        edge_state,
        senders.reshape(1, faces),
        receivers.reshape(1, faces),
        node_cotangent,
        edge_cotangent,
        edge_first.T,
        edge_second,
        node_first.T,
        node_second,
        vectors,
    )
    returned, forth, back = exchange(ghost)
    further, nearer = shift(forth, 1), shift(back, -1)
    totals = total_over(partial)
    state, edgefirst, edgesecond, nodefirst, nodesecond, vector = pl.pallas_call(
        final_kernel,
        out_shape=(
            shape((features, cells), BF16),
            shape((features, 3 * features), F32),
            shape((features, features), F32),
            shape((features, 2 * features), F32),
            shape((features, features), F32),
            shape((VECTORS, features), F32),
        ),
        name="final",
    )(local, returned, further, nearer, index, totals)
    return (
        state,
        edge_result,
        edgefirst.T,
        vector[0],
        edgesecond,
        vector[1],
        vector[2],
        nodefirst.T,
        vector[3],
        nodesecond,
        vector[4],
        vector[5],
    )


def solution(mesh):
    parts = ("dom", "sub")
    columns = P(None, parts)
    in_specs = (columns, columns, P(parts), P(parts), P(parts, None, None), columns, columns)
    in_specs = in_specs + (P(),) * 9
    out_specs = (columns, columns) + (P(),) * 10
    return jax.shard_map(
        on_device, mesh=mesh, in_specs=in_specs, out_specs=out_specs, check_vma=False
    )
```

time: 291 us -> 72.9 us (0.25)
  waiting for transfers between devices: 136 us -> 16.7 us
  matrix products: 92.7 us -> 0 us
  other arithmetic: 20.3 us -> 0.73 us
  Pallas kernels: 0 us -> 14.8 us
  between operations: 14.6 us -> 0.84 us
  blocking collectives: 0 us -> 9.68 us
  starting transfers between devices: 18.7 us -> 21.9 us
    psum x1 -> x0, waiting for transfers between devices: 125 us -> none  [on_device(): lax.psum((partials[0], partials[1], partials[2], partials[3], partials[4]...]
    dot_general x102 -> x0, matrix products: 92.7 us -> none  [the longest x45 56.2 us: one_block(): jnp.dot(portion, selector, precision=precision, preferred_element_type=jn...]
    ppermute x4 -> x9, waiting for transfers between devices: 1.69 us -> 16.7 us  [the longest x5 11.9 us: total_over(): lax.ppermute(value, axis, [(i, i ^ step) for i in range(count)])]
    pallas_call x0 -> x3, Pallas kernels: none -> 14.8 us  [the longest x1 10.6 us: on_device(): pl.pallas_call(functools.partial(main_kernel, tile=tile, factor=factor),...]
    mul x10 -> x0, other arithmetic: 12.4 us -> none  [the longest x1 1.47 us: on_device(): edgefirst_sum * factor]
    all_to_all x0 -> x1, blocking collectives: none -> 9.68 us  [exchange(): lax.all_to_all(blocks, 'sub', split_axis=0, concat_axis=0, tiled=True)]
    all_to_all x2 -> x1, waiting for transfers between devices: 9.44 us -> 0.01 us  [exchange(): lax.all_to_all(blocks, 'sub', split_axis=0, concat_axis=0, tiled=True)]
    ppermute x4 -> x9, starting transfers between devices: 11.1 us -> 18.5 us  [the longest x4 11.3 us: shift(): lax.ppermute(value, 'dom', [(source, source + steps) for source in range(...]
  transfers between devices with their start and end apart: 7 -> 10, of which waited for: 4 -> 7; matrix products, arithmetic and copies ran while one was open for 7% -> 1% of each run, Pallas kernels for 0% -> 0%
where the time goes in v1:
time: 72.9 us; the launch traced here: 71.8 us
  starting transfers between devices  21.9 us (30%)
  waiting for transfers between devices  16.7 us (23%)
  Pallas kernels  14.8 us (20%)
  blocking collectives  9.68 us (13%)
  local copies, waits for them, and re-layouts  7.14 us (10%)
  between operations  0.84 us (1%)
  other arithmetic  0.73 us (1%)
    ppermute x5, waiting for transfers between devices, total_over(): lax.ppermute(value, axis, [(i, i ^ step) for i in range(count)])  11.9 us
    ppermute x4, starting transfers between devices, shift(): lax.ppermute(value, 'dom', [(source, source + steps) for source in range(...  11.3 us
    pallas_call x1, Pallas kernels, on_device(): pl.pallas_call(functools.partial(main_kernel, tile=tile, factor=factor),...  10.6 us
    all_to_all x1, blocking collectives, exchange(): lax.all_to_all(blocks, 'sub', split_axis=0, concat_axis=0, tiled=True)  9.68 us
    ppermute x5, starting transfers between devices, total_over(): lax.ppermute(value, axis, [(i, i ^ step) for i in range(count)])  7.22 us
    unnamed x39, local copies, waits for them, and re-layouts  5.56 us
    ppermute x4, waiting for transfers between devices, shift(): lax.ppermute(value, 'dom', [(source, source + steps) for source in range(...  4.85 us
    all_to_all x1, starting transfers between devices, exchange(): lax.all_to_all(blocks, 'sub', split_axis=0, concat_axis=0, tiled=True)  3.36 us
  transfers between devices with their start and end apart: 10, of which 7 were waited for; matrix products, arithmetic and copies ran while one was open for 1% of the time, Pallas kernels for 0%

profile of v1, /device:TPU:0, one launch (start us, length us, event | category | flops | bytes accessed | tf_op | source)
XLA Modules:
  0.0 71.8 jit_solution(3000767998067638896)
XLA Ops:
  0.7 1.3 %copy.48 = s32[1,12,128]{2,1,0:T(8,128)} copy(s32[1,12,128]{2,0,1:T(1,128)} %param.20) | data formatting | bytes 12288
  1.9 2.0 %pick.1 = bf16[4,3,64,128]{3,2,1,0:T(8,128)(2,1)} custom-call(bf16[64,1024]{1,0:T(8,128)(2,1)} %node_ref.3, s32[12,128]{1,0:T(8,128)} %bitcast.46), custom_call_target="tpu_custom_call" | custom-call | tf_op jit(solution)/shard_map/pick/pallas_call | solution.py:364
  4.0 9.7 %all_to_all.10.across_ref = bf16[4,3,64,128]{3,2,1,0:T(8,128)(2,1)S(1)} all-to-all(bf16[4,3,64,128]{3,2,1,0:T(8,128)(2,1)} %pick.1), channel_id=1, replica_groups=mesh['dom'=8,'sub'=4] {'sub'}, dimensions={0} | all-to-all | bytes 393216 | tf_op jit(solution)/shard_map/all_to_all | solution.py:316
  13.7 4.1 %collective-permute-start.1 = (bf16[4,64,128]{2,1,0:T(8,128)(2,1)S(1)}, bf16[4,64,128]{2,1,0:T(8,128)(2,1)S(1)}, u32[]{:S(2)}, u32[]{:S(2)}) collective-permute-start(bf16[4,64,128]{2,1,0:T(8,128)(2,1)S(1)} %get-tuple-element.34), channel_id=1, source_target_pairs={{0,4},{4,8},{8,12},{12,16},{16,20},{20,24},{24,28},{1,5},{5,9},{9,... | collective-permute-start | bytes 196616 | tf_op jit(solution)/shard_map/ppermute | solution.py:312
  17.8 1.3 %collective-permute-start = (bf16[4,64,128]{2,1,0:T(8,128)(2,1)S(1)}, bf16[4,64,128]{2,1,0:T(8,128)(2,1)S(1)}, u32[]{:S(2)}, u32[]{:S(2)}) collective-permute-start(bf16[4,64,128]{2,1,0:T(8,128)(2,1)S(1)} %get-tuple-element.35), channel_id=1, source_target_pairs={{4,0},{8,4},{12,8},{16,12},{20,16},{24,20},{28,24},{5,1},{9,5},{13... | collective-permute-start | bytes 196616 | tf_op jit(solution)/shard_map/ppermute | solution.py:312
  19.7 4.3 %collective-permute-done.upper_ref = bf16[4,64,128]{2,1,0:T(8,128)(2,1)S(1)} collective-permute-done((bf16[4,64,128]{2,1,0:T(8,128)(2,1)S(1)}, bf16[4,64,128]{2,1,0:T(8,128)(2,1)S(1)}, u32[]{:S(2)}, u32[]{:S(2)}) %collective-permute-start) | collective-permute-done | bytes 65568 | tf_op jit(solution)/shard_map/ppermute | solution.py:312
  24.0 0.7 %copy-done.5 = bf16[192,64]{0,1:T(8,128)(2,1)S(1)} copy-done((bf16[192,64]{0,1:T(8,128)(2,1)S(1)}, bf16[192,64]{0,1:T(8,128)(2,1)}, u32[]{:S(2)}) %copy-start.5) | copy-done | bytes 24600
  24.8 0.7 copy-done.7
  25.5 0.7 copy-done.8
  26.2 0.7 copy-done.9
  26.9 0.7 copy-done.10
  27.6 10.6 %main.1 = (f32[64,1024]{1,0:T(8,128)S(1)}, bf16[4,3,64,128]{3,2,1,0:T(8,128)(2,1)}, bf16[64,3072]{1,0:T(8,128)(2,1)}, f32[256,128]{1,0:T(8,128)S(1)}) custom-call(bf16[64,1024]{1,0:T(8,128)(2,1)S(1)} %copy-done, bf16[4,3,64,128]{3,2,1,0:T(8,128)(2,1)S(1)} %all_to_all.10.across_ref, bf16[4,64,128]{2,1,0:T(8,128)(2,1)S(1)} %collective-permute-done.upper_ref, ...), custom_call_target="tpu_custom_call" | custom-call | tf_op jit(solution)/shard_map/main/pallas_call | solution.py:368
  38.2 1.3 %collective-permute-done.4 = f32[256,128]{1,0:T(8,128)S(1)} collective-permute-done((f32[256,128]{1,0:T(8,128)S(1)}, f32[256,128]{1,0:T(8,128)S(1)}, u32[]{:S(2)}, u32[]{:S(2)}) %collective-permute-start.4) | collective-permute-done | bytes 131104 | tf_op jit(solution)/shard_map/ppermute | solution.py:328
  40.0 5.2 %collective-permute-done.5 = f32[256,128]{1,0:T(8,128)S(1)} collective-permute-done((f32[256,128]{1,0:T(8,128)S(1)}, f32[256,128]{1,0:T(8,128)S(1)}, u32[]{:S(2)}, u32[]{:S(2)}) %collective-permute-start.5) | collective-permute-done | bytes 131104 | tf_op jit(solution)/shard_map/ppermute | solution.py:328
  45.2 2.5 %collective-permute-start.6 = (f32[256,128]{1,0:T(8,128)S(1)}, f32[256,128]{1,0:T(8,128)S(1)}, u32[]{:S(2)}, u32[]{:S(2)}) collective-permute-start(f32[256,128]{1,0:T(8,128)S(1)} %add.16), channel_id=1, source_target_pairs={{0,4},{4,0},{8,12},{12,8},{16,20},{20,16},{24,28},{28,24},{1,5},{5... | collective-permute-start | bytes 393224 | tf_op jit(solution)/shard_map/ppermute | solution.py:328
  47.7 3.4 %all-to-all-start.1 = ((bf16[4,3,64,128]{3,2,1,0:T(8,128)(2,1)}), bf16[4,3,64,128]{3,2,1,0:T(8,128)(2,1)S(1)}, u32[]{:S(2)}, u32[]{:S(2)}) async-start(bf16[4,3,64,128]{3,2,1,0:T(8,128)(2,1)} %get-tuple-element.23), calls=%async_computation.1 | async-start | bytes 393216 | tf_op jit(solution)/shard_map/all_to_all | solution.py:316
  51.1 1.6 %collective-permute-start.7 = (f32[256,128]{1,0:T(8,128)S(1)}, f32[256,128]{1,0:T(8,128)S(1)}, u32[]{:S(2)}, u32[]{:S(2)}) collective-permute-start(f32[256,128]{1,0:T(8,128)S(1)} %add.17), channel_id=1, source_target_pairs={{0,8},{4,12},{8,0},{12,4},{16,24},{20,28},{24,16},{28,20},{1,9},{5... | collective-permute-start | bytes 393224 | tf_op jit(solution)/shard_map/ppermute | solution.py:328
  52.8 4.3 %collective-permute-done.7 = f32[256,128]{1,0:T(8,128)S(1)} collective-permute-done((f32[256,128]{1,0:T(8,128)S(1)}, f32[256,128]{1,0:T(8,128)S(1)}, u32[]{:S(2)}, u32[]{:S(2)}) %collective-permute-start.7) | collective-permute-done | bytes 131104 | tf_op jit(solution)/shard_map/ppermute | solution.py:328
  57.1 2.6 %collective-permute-start.8 = (f32[256,128]{1,0:T(8,128)S(1)}, f32[256,128]{1,0:T(8,128)S(1)}, u32[]{:S(2)}, u32[]{:S(2)}) collective-permute-start(f32[256,128]{1,0:T(8,128)S(1)} %add.18), channel_id=1, source_target_pairs={{0,16},{4,20},{8,24},{12,28},{16,0},{20,4},{24,8},{28,12},{1,17},{... | collective-permute-start | bytes 393224 | tf_op jit(solution)/shard_map/ppermute | solution.py:328
  59.7 1.3 %collective-permute-start.3 = (bf16[4,64,128]{2,1,0:T(8,128)(2,1)S(1)}, bf16[4,64,128]{2,1,0:T(8,128)(2,1)S(1)}, u32[]{:S(2)}, u32[]{:S(2)}) collective-permute-start(bf16[4,64,128]{2,1,0:T(8,128)(2,1)S(1)} %get-tuple-element.32), channel_id=1, source_target_pairs={{4,0},{8,4},{12,8},{16,12},{20,16},{24,20},{28,24},{5,1},{9,5},{13... | collective-permute-start | bytes 196616 | tf_op jit(solution)/shard_map/ppermute | solution.py:312
  61.0 4.5 %collective-permute-start.2 = (bf16[4,64,128]{2,1,0:T(8,128)(2,1)S(1)}, bf16[4,64,128]{2,1,0:T(8,128)(2,1)S(1)}, u32[]{:S(2)}, u32[]{:S(2)}) collective-permute-start(bf16[4,64,128]{2,1,0:T(8,128)(2,1)S(1)} %get-tuple-element.33), channel_id=1, source_target_pairs={{0,4},{4,8},{8,12},{12,16},{16,20},{20,24},{24,28},{1,5},{5,9},{9,... | collective-permute-start | bytes 196616 | tf_op jit(solution)/shard_map/ppermute | solution.py:312
  65.6 1.1 %collective-permute-done.8 = f32[256,128]{1,0:T(8,128)S(1)} collective-permute-done((f32[256,128]{1,0:T(8,128)S(1)}, f32[256,128]{1,0:T(8,128)S(1)}, u32[]{:S(2)}, u32[]{:S(2)}) %collective-permute-start.8) | collective-permute-done | bytes 131104 | tf_op jit(solution)/shard_map/ppermute | solution.py:328
  68.1 2.2 %final.1 = (bf16[64,1024]{1,0:T(8,128)(2,1)}, f32[64,192]{1,0:T(8,128)}, f32[64,64]{1,0:T(8,128)}, f32[64,128]{1,0:T(8,128)}, f32[64,64]{1,0:T(8,128)}, /*index=5*/f32[6,64]{1,0:T(8,128)}) custom-call(f32[64,1024]{1,0:T(8,128)} %copy-done.3, bf16[4,3,64,128]{3,2,1,0:T(8,128)(2,1)} %copy-done.11, bf16[4,64,128]{2,1,0:T(8,128)(2,1)} %copy-done.13, ...), custom_call_target="tpu_custom_call" | custom-call | tf_op jit(solution)/shard_map/final/pallas_call | solution.py:406
  70.3 1.4 %slice_bitcast_fusion.4 = (f32[64]{0:T(128)}, f32[64]{0:T(128)}, f32[64]{0:T(128)}, f32[64]{0:T(128)}, f32[64]{0:T(128)}, /*index=5*/f32[64]{0:T(128)}) fusion(f32[6,64]{1,0:T(8,128)} %get-tuple-element.28), kind=kLoop, calls=%fused_computation.5 | loop fusion | bytes 3072 | tf_op jit(solution)/shard_map/squeeze | solution.py:430
  (49 shorter events, 2.6 us)
Async XLA Ops:
  0.6 23.4 %copy-start.6 = (bf16[64,64]{1,0:T(8,128)(2,1)S(1)}, bf16[64,64]{1,0:T(8,128)(2,1)}, u32[]{:S(2)}) copy-start(bf16[64,64]{1,0:T(8,128)(2,1)} %edgesecond_ref.1) | copy-start | bytes 24580
  1.9 22.1 %copy-start.2 = (bf16[64,3072]{1,0:T(8,128)(2,1)S(1)}, bf16[64,3072]{1,0:T(8,128)(2,1)}, u32[]{:S(2)}) copy-start(bf16[64,3072]{1,0:T(8,128)(2,1)} %edgecot_ref.1) | copy-start | bytes 1179652
  4.0 15.2 %copy-start.14 = (f32[64]{0:T(128)S(1)}, f32[64]{0:T(128)}, u32[]{:S(2)}) copy-start(f32[64]{0:T(128)} %param.24) | copy-start | bytes 772
  4.0 15.2 %copy-start.15 = (f32[64]{0:T(128)S(1)}, f32[64]{0:T(128)}, u32[]{:S(2)}) copy-start(f32[64]{0:T(128)} %param.26) | copy-start | bytes 772
  4.0 15.2 %copy-start.16 = (f32[64]{0:T(128)S(1)}, f32[64]{0:T(128)}, u32[]{:S(2)}) copy-start(f32[64]{0:T(128)} %param.27) | copy-start | bytes 772
  4.0 15.2 %copy-start.17 = (f32[64]{0:T(128)S(1)}, f32[64]{0:T(128)}, u32[]{:S(2)}) copy-start(f32[64]{0:T(128)} %param.29) | copy-start | bytes 772
  4.0 15.2 %copy-start.18 = (f32[64]{0:T(128)S(1)}, f32[64]{0:T(128)}, u32[]{:S(2)}) copy-start(f32[64]{0:T(128)} %param.31) | copy-start | bytes 772
  4.0 20.0 %copy-start.1 = (bf16[64,3072]{1,0:T(8,128)(2,1)S(1)}, bf16[64,3072]{1,0:T(8,128)(2,1)}, u32[]{:S(2)}) copy-start(bf16[64,3072]{1,0:T(8,128)(2,1)} %edge_ref.1) | copy-start | bytes 1179652
  13.7 10.3 %copy-start = (bf16[64,1024]{1,0:T(8,128)(2,1)S(1)}, bf16[64,1024]{1,0:T(8,128)(2,1)}, u32[]{:S(2)}) copy-start(bf16[64,1024]{1,0:T(8,128)(2,1)} %node_ref.3) | copy-start | bytes 393220
  13.7 10.3 %copy-start.4 = (bf16[64,1024]{1,0:T(8,128)(2,1)S(1)}, bf16[64,1024]{1,0:T(8,128)(2,1)}, u32[]{:S(2)}) copy-start(bf16[64,1024]{1,0:T(8,128)(2,1)} %nodecot_ref.1) | copy-start | bytes 393220
  13.7 6.0 %collective-permute-start.1 = (bf16[4,64,128]{2,1,0:T(8,128)(2,1)S(1)}, bf16[4,64,128]{2,1,0:T(8,128)(2,1)S(1)}, u32[]{:S(2)}, u32[]{:S(2)}) collective-permute-start(bf16[4,64,128]{2,1,0:T(8,128)(2,1)S(1)} %get-tuple-element.34), channel_id=1, source_target_pairs={{0,4},{4,8},{8,12},{12,16},{16,20},{20,24},{24,28},{1,5},{5,9},{9,... | collective-permute-start | bytes 196616 | tf_op jit(solution)/shard_map/ppermute | solution.py:312
  17.8 6.2 %collective-permute-start = (bf16[4,64,128]{2,1,0:T(8,128)(2,1)S(1)}, bf16[4,64,128]{2,1,0:T(8,128)(2,1)S(1)}, u32[]{:S(2)}, u32[]{:S(2)}) collective-permute-start(bf16[4,64,128]{2,1,0:T(8,128)(2,1)S(1)} %get-tuple-element.35), channel_id=1, source_target_pairs={{4,0},{8,4},{12,8},{16,12},{20,16},{24,20},{28,24},{5,1},{9,5},{13... | collective-permute-start | bytes 196616 | tf_op jit(solution)/shard_map/ppermute | solution.py:312
  24.0 0.8 %copy-start.5 = (bf16[192,64]{0,1:T(8,128)(2,1)S(1)}, bf16[192,64]{0,1:T(8,128)(2,1)}, u32[]{:S(2)}) copy-start(bf16[192,64]{0,1:T(8,128)(2,1)} %param.23) | copy-start | bytes 73732
  24.8 0.7 copy-start.7
  38.2 7.0 %copy-start.3 = (f32[64,1024]{1,0:T(8,128)}, f32[64,1024]{1,0:T(8,128)S(1)}, u32[]{:S(2)}) copy-start(f32[64,1024]{1,0:T(8,128)S(1)} %get-tuple-element.22.local_ref) | copy-start | bytes 786436
  38.2 1.3 %collective-permute-start.4 = (f32[256,128]{1,0:T(8,128)S(1)}, f32[256,128]{1,0:T(8,128)S(1)}, u32[]{:S(2)}, u32[]{:S(2)}) collective-permute-start(f32[256,128]{1,0:T(8,128)S(1)} %get-tuple-element.24), channel_id=1, source_target_pairs={{0,1},{1,0},{2,3},{3,2},{4,5},{5,4},{6,7},{7,6},{8,9},{9,8},{10,11... | collective-permute-start | bytes 393224 | tf_op jit(solution)/shard_map/ppermute | solution.py:328
  39.6 5.6 %collective-permute-start.5 = (f32[256,128]{1,0:T(8,128)S(1)}, f32[256,128]{1,0:T(8,128)S(1)}, u32[]{:S(2)}, u32[]{:S(2)}) collective-permute-start(f32[256,128]{1,0:T(8,128)S(1)} %add.15), channel_id=1, source_target_pairs={{0,2},{1,3},{2,0},{3,1},{4,6},{5,7},{6,4},{7,5},{8,10},{9,11},{10,... | collective-permute-start | bytes 393224 | tf_op jit(solution)/shard_map/ppermute | solution.py:328
  45.2 5.9 %collective-permute-start.6 = (f32[256,128]{1,0:T(8,128)S(1)}, f32[256,128]{1,0:T(8,128)S(1)}, u32[]{:S(2)}, u32[]{:S(2)}) collective-permute-start(f32[256,128]{1,0:T(8,128)S(1)} %add.16), channel_id=1, source_target_pairs={{0,4},{4,0},{8,12},{12,8},{16,20},{20,16},{24,28},{28,24},{1,5},{5... | collective-permute-start | bytes 393224 | tf_op jit(solution)/shard_map/ppermute | solution.py:328
  47.7 12.0 %all-to-all-start.1 = ((bf16[4,3,64,128]{3,2,1,0:T(8,128)(2,1)}), bf16[4,3,64,128]{3,2,1,0:T(8,128)(2,1)S(1)}, u32[]{:S(2)}, u32[]{:S(2)}) async-start(bf16[4,3,64,128]{3,2,1,0:T(8,128)(2,1)} %get-tuple-element.23), calls=%async_computation.1 | async-start | bytes 393216 | tf_op jit(solution)/shard_map/all_to_all | solution.py:316
  51.1 5.9 %collective-permute-start.7 = (f32[256,128]{1,0:T(8,128)S(1)}, f32[256,128]{1,0:T(8,128)S(1)}, u32[]{:S(2)}, u32[]{:S(2)}) collective-permute-start(f32[256,128]{1,0:T(8,128)S(1)} %add.17), channel_id=1, source_target_pairs={{0,8},{4,12},{8,0},{12,4},{16,24},{20,28},{24,16},{28,20},{1,9},{5... | collective-permute-start | bytes 393224 | tf_op jit(solution)/shard_map/ppermute | solution.py:328
  57.1 9.6 %collective-permute-start.8 = (f32[256,128]{1,0:T(8,128)S(1)}, f32[256,128]{1,0:T(8,128)S(1)}, u32[]{:S(2)}, u32[]{:S(2)}) collective-permute-start(f32[256,128]{1,0:T(8,128)S(1)} %add.18), channel_id=1, source_target_pairs={{0,16},{4,20},{8,24},{12,28},{16,0},{20,4},{24,8},{28,12},{1,17},{... | collective-permute-start | bytes 393224 | tf_op jit(solution)/shard_map/ppermute | solution.py:328
  59.7 7.6 %copy-start.11 = (bf16[4,3,64,128]{3,2,1,0:T(8,128)(2,1)}, bf16[4,3,64,128]{3,2,1,0:T(8,128)(2,1)S(1)}, u32[]{:S(2)}) copy-start(bf16[4,3,64,128]{3,2,1,0:T(8,128)(2,1)S(1)} %all-to-all-done.1.across_ref) | copy-start | bytes 589828
  59.7 7.6 %collective-permute-start.3 = (bf16[4,64,128]{2,1,0:T(8,128)(2,1)S(1)}, bf16[4,64,128]{2,1,0:T(8,128)(2,1)S(1)}, u32[]{:S(2)}, u32[]{:S(2)}) collective-permute-start(bf16[4,64,128]{2,1,0:T(8,128)(2,1)S(1)} %get-tuple-element.32), channel_id=1, source_target_pairs={{4,0},{8,4},{12,8},{16,12},{20,16},{24,20},{28,24},{5,1},{9,5},{13... | collective-permute-start | bytes 196616 | tf_op jit(solution)/shard_map/ppermute | solution.py:312
  61.0 6.4 %collective-permute-start.2 = (bf16[4,64,128]{2,1,0:T(8,128)(2,1)S(1)}, bf16[4,64,128]{2,1,0:T(8,128)(2,1)S(1)}, u32[]{:S(2)}, u32[]{:S(2)}) collective-permute-start(bf16[4,64,128]{2,1,0:T(8,128)(2,1)S(1)} %get-tuple-element.33), channel_id=1, source_target_pairs={{0,4},{4,8},{8,12},{12,16},{16,20},{20,24},{24,28},{1,5},{5,9},{9,... | collective-permute-start | bytes 196616 | tf_op jit(solution)/shard_map/ppermute | solution.py:312
  (5 other events, 3.4 us)

commit v2 on v1

--- a/solution.py
+++ b/solution.py
@@ -78,13 +78,13 @@
 
 
 def pair_rows(index_ref, first):
-    return jnp.concatenate([index_ref[first : first + 1], index_ref[first + 1 : first + 2]], axis=1)
+    return jnp.concatenate([index_ref[first], index_ref[first + 1]], axis=1)
 
 
 def pick_kernel(node_ref, index_ref, out_ref):
     features = node_ref.shape[0]
     subs = out_ref.shape[0]
-    halo = index_ref.shape[1]
+    halo = index_ref.shape[2]
     table = stack_table(node_ref[...])
     for first in range(0, index_ref.shape[0], 2):
         index = pair_rows(index_ref, first)
@@ -94,12 +94,48 @@
             out_ref[block % subs, block // subs] = chosen[:, extra * halo : (extra + 1) * halo]
 
 
+def fill_table(table_ref, node_state, across_ref, upper_ref, lower_ref):
+    features, cells = node_state.shape
+    subs, halo = upper_ref.shape[0], upper_ref.shape[2]
+    own = cells // LOW
+    table_ref[: own * features] = stack_table(node_state)
+    for block in range(3 * subs):
+        source = (
+            upper_ref[block % subs]
+            if block < subs
+            else (across_ref[block % subs, 1] if block < 2 * subs else lower_ref[block % subs])
+        )
+        column = block * halo
+        row = (own + column // LOW) * features
+        table_ref[row : row + features, column % LOW : column % LOW + halo] = source
+
+
+def flip(matrix):
+    return matrix.astype(F32).T.astype(BF16)
+
+
+def early_kernel(
+    node_ref, edge_ref, senders_ref, receivers_ref, edgefirst_ref, vectors_ref, linear_ref, *, tile
+):
+    features = node_ref.shape[0]
+    table = stack_table(node_ref[...])
+    first_t = edgefirst_ref[...]
+    edge_bias = vectors_ref[:, 0:1]
+    for begin in range(0, edge_ref.shape[1], tile):
+        at = slice(begin, begin + tile)
+        sender, receiver = senders_ref[:, at], receivers_ref[:, at]
+        sender_rows = pick_high(mm(table, low_hot(sender)), sender, features).astype(BF16)
+        receiver_rows = pick_high(mm(table, low_hot(receiver)), receiver, features).astype(BF16)
+        stacked = jnp.concatenate([sender_rows, receiver_rows, edge_ref[:, at]], axis=0)
+        linear_ref[:, at] = mm(first_t, stacked) + edge_bias
+
+
 def main_kernel(
+    linear_ref,
     node_ref,
     across_ref,
     upper_ref,
     lower_ref,
-    edge_ref,
     senders_ref,
     receivers_ref,
     nodecot_ref,
@@ -109,15 +145,17 @@
     nodefirst_ref,
     nodesecond_ref,
     vectors_ref,
+    ghost_ref,
     local_ref,
-    ghost_ref,
-    result_ref,
+    sum_ref,
+    active_ref,
+    delta_ref,
+    hidden_ref,
     partial_ref,
     table_ref,
     shot_ref,
     rhot_ref,
     slope_ref,
-    active_ref,
     scaled_ref,
     spread_ref,
     *,
@@ -125,30 +163,20 @@
     factor,
 ):
     features, cells = node_ref.shape
-    faces = edge_ref.shape[1]
+    faces = senders_ref.shape[1]
     subs, halo = upper_ref.shape[0], upper_ref.shape[2]
     own = cells // LOW
     total = table_ref.shape[0] // features
     vectors = vectors_ref[...]
-    edge_bias, edge_gain, edge_shift, node_bias, node_gain = [
-        vectors[:, number : number + 1] for number in range(5)
+    edge_gain, edge_shift, node_bias, node_gain = [
+        vectors[:, number : number + 1] for number in range(1, 5)
     ]
-    first_t = edgefirst_ref[...]
+    first_st = edgefirst_ref[:, :features]
     second = edgesecond_ref[...]
-    second_t = second.astype(F32).T.astype(BF16)
-    first = first_t.astype(F32).T.astype(BF16)
-
+    second_t = flip(second)
+    first_s = flip(first_st)
     node_state = node_ref[...]
-    table_ref[: own * features] = stack_table(node_state)
-    for block in range(3 * subs):
-        source = (
-            upper_ref[block % subs]
-            if block < subs
-            else (across_ref[block % subs, 1] if block < 2 * subs else lower_ref[block % subs])
-        )
-        column = block * halo
-        row = (own + column // LOW) * features
-        table_ref[row : row + features, column % LOW : column % LOW + halo] = source
+    fill_table(table_ref, node_state, across_ref, upper_ref, lower_ref)
 
     summed = jnp.zeros((own * features, LOW), F32)
     for begin in range(0, faces, tile):
@@ -157,12 +185,10 @@
         shot, rhot = low_hot(sender), low_hot(receiver)
         shot_ref[:, at] = shot
         rhot_ref[:, at] = rhot
-        sender_rows = pick_high(mm(table_ref[...], shot), sender, features).astype(BF16)
-        receiver_rows = pick_high(
-            mm(table_ref[: own * features], rhot), receiver, features
+        ghost_rows = pick_high(
+            mm(table_ref[own * features :], shot), sender - cells, features
         ).astype(BF16)
-        stacked = jnp.concatenate([sender_rows, receiver_rows, edge_ref[:, at]], axis=0)
-        linear = mm(first_t, stacked) + edge_bias
+        linear = linear_ref[:, at] + mm(first_st, ghost_rows)
         logistic = sigmoid(linear)
         slope_ref[:, at] = logistic * (1.0 + linear * (1.0 - logistic))
         active = (linear * logistic).astype(BF16)
@@ -174,9 +200,9 @@
         summed = summed + mm_nt(spread_high(message, receiver, own), rhot)
 
     node_first_t = nodefirst_ref[...]
-    node_first = node_first_t.astype(F32).T.astype(BF16)
+    node_first = flip(node_first_t)
     node_second = nodesecond_ref[...]
-    node_second_t = node_second.astype(F32).T.astype(BF16)
+    node_second_t = flip(node_second)
     node_input = jnp.concatenate([node_state, unstack(summed, features).astype(BF16)], axis=0)
     node_linear = mm(node_first_t, node_input) + node_bias
     node_logistic = sigmoid(node_linear)
@@ -198,44 +224,32 @@
     back_table = stack_table(node_back[features:]).astype(BF16)
 
     sender_sum = jnp.zeros((total * features, LOW), F32)
-    receiver_sum = jnp.zeros((own * features, LOW), F32)
     gain_sum = jnp.zeros((features, tile), F32)
     shift_sum = jnp.zeros((features, tile), F32)
     bias_sum = jnp.zeros((features, tile), F32)
-    edgesecond_delta = jnp.zeros((features, features), F32)
-    edgethird_delta = jnp.zeros((features, features), F32)
-    first_s, first_r, first_e = [
-        first[number * features : (number + 1) * features] for number in range(3)
-    ]
     for begin in range(0, faces, tile):
         at = slice(begin, begin + tile)
         sender, receiver = senders_ref[:, at], receivers_ref[:, at]
-        shot, rhot = shot_ref[:, at], rhot_ref[:, at]
-        cotangent = edgecot_ref[:, at].astype(F32)
         scaled = scaled_ref[:, at]
-        message_delta = cotangent + pick_high(mm(back_table, rhot), receiver, features)
+        message_delta = edgecot_ref[:, at].astype(F32) + pick_high(
+            mm(back_table, rhot_ref[:, at]), receiver, features
+        )
         gain_sum = gain_sum + message_delta * scaled
         shift_sum = shift_sum + message_delta
         delta = norm_back(message_delta, scaled, spread_ref[:, at], edge_gain).astype(BF16)
-        edgesecond_delta = edgesecond_delta + mm_nt(active_ref[:, at], delta)
+        delta_ref[:, at] = delta
         hidden = mm(second, delta) * slope_ref[:, at]
         bias_sum = bias_sum + hidden
         rounded = hidden.astype(BF16)
-        result_ref[:, at] = (cotangent + mm(first_e, rounded)).astype(BF16)
-        edgethird_delta = edgethird_delta + mm_nt(edge_ref[:, at], rounded)
-        wide = rounded.astype(F32)
-        sender_sum = sender_sum + mm_nt(spread_high(wide, sender, total), shot)
-        receiver_sum = receiver_sum + mm_nt(spread_high(wide, receiver, own), rhot)
+        hidden_ref[:, at] = rounded
+        sender_sum = sender_sum + mm_nt(
+            spread_high(rounded.astype(F32), sender, total), shot_ref[:, at]
+        )
 
     sender_sum = sender_sum.astype(BF16)
-    receiver_sum = unstack(receiver_sum, features).astype(BF16)
-    edgefirst_s = jnp.zeros((features, features), F32)
-    for number in range(total):
-        rows = slice(number * features, (number + 1) * features)
-        edgefirst_s = edgefirst_s + mm_nt(table_ref[rows], sender_sum[rows])
-    edgefirst_r = mm_nt(node_state, receiver_sum)
+    sum_ref[...] = sender_sum
     spread_out = mm(first_s, unstack(sender_sum, features))
-    local_ref[...] = local + spread_out[:, :cells] + mm(first_r, receiver_sum)
+    local_ref[...] = local + spread_out[:, :cells]
     for block in range(3 * subs):
         column = cells + block * halo
         ghost_ref[block % subs, block // subs] = spread_out[:, column : column + halo].astype(BF16)
@@ -253,8 +267,6 @@
     for number, column in enumerate(columns):
         vector_block = jnp.where(lanes == number, column, vector_block)
     pairs = (
-        (edgefirst_s, edgefirst_r),
-        (edgethird_delta, edgesecond_delta),
         (nodefirst_delta[:features], nodefirst_delta[features:]),
         (nodesecond_delta, vector_block),
     )
@@ -262,6 +274,65 @@
         partial_ref[number * features : (number + 1) * features] = (
             jnp.concatenate([left, right], axis=1) * factor
         )
+
+
+def late_kernel(
+    local_ref,
+    sum_ref,
+    active_ref,
+    delta_ref,
+    hidden_ref,
+    node_partial_ref,
+    node_ref,
+    across_ref,
+    upper_ref,
+    lower_ref,
+    edge_ref,
+    receivers_ref,
+    edgecot_ref,
+    edgefirst_ref,
+    partial_ref,
+    result_ref,
+    state_ref,
+    table_ref,
+    *,
+    tile,
+    factor,
+):
+    features, cells = node_ref.shape
+    faces = edge_ref.shape[1]
+    own = cells // LOW
+    total = table_ref.shape[0] // features
+    node_state = node_ref[...]
+    fill_table(table_ref, node_state, across_ref, upper_ref, lower_ref)
+    first = flip(edgefirst_ref[...])
+    first_r, first_e = first[features : 2 * features], first[2 * features :]
+    receiver_sum = jnp.zeros((own * features, LOW), F32)
+    edgesecond_delta = jnp.zeros((features, features), F32)
+    edgethird_delta = jnp.zeros((features, features), F32)
+    for begin in range(0, faces, tile):
+        at = slice(begin, begin + tile)
+        receiver = receivers_ref[:, at]
+        rounded = hidden_ref[:, at]
+        edgesecond_delta = edgesecond_delta + mm_nt(active_ref[:, at], delta_ref[:, at])
+        edgethird_delta = edgethird_delta + mm_nt(edge_ref[:, at], rounded)
+        result_ref[:, at] = (edgecot_ref[:, at].astype(F32) + mm(first_e, rounded)).astype(BF16)
+        receiver_sum = receiver_sum + mm_nt(
+            spread_high(rounded.astype(F32), receiver, own), low_hot(receiver)
+        )
+    receiver_sum = unstack(receiver_sum, features).astype(BF16)
+    edgefirst_s = jnp.zeros((features, features), F32)
+    for number in range(total):
+        rows = slice(number * features, (number + 1) * features)
+        edgefirst_s = edgefirst_s + mm_nt(table_ref[rows], sum_ref[rows])
+    edgefirst_r = mm_nt(node_state, receiver_sum)
+    state_ref[...] = local_ref[...] + mm(first_r, receiver_sum)
+    pairs = ((edgefirst_s, edgefirst_r), (edgethird_delta, edgesecond_delta))
+    for number, (left, right) in enumerate(pairs):
+        partial_ref[number * features : (number + 1) * features] = (
+            jnp.concatenate([left, right], axis=1) * factor
+        )
+    partial_ref[2 * features :] = node_partial_ref[...]
 
 
 def final_kernel(
@@ -276,7 +347,7 @@
     edgesecond_ref,
     nodefirst_ref,
     nodesecond_ref,
-    vector_ref,
+    *vector_refs,
 ):
     features, cells = local_ref.shape
     subs = further_ref.shape[0]
@@ -303,7 +374,9 @@
     edgesecond_ref[...] = halves[1][1]
     nodefirst_ref[...] = jnp.concatenate([halves[2][0], halves[2][1]], axis=0).T
     nodesecond_ref[...] = halves[3][0]
-    vector_ref[...] = halves[3][1].T[: vector_ref.shape[0]]
+    rows = halves[3][1].T
+    for number, vector_ref in enumerate(vector_refs):
+        vector_ref[...] = rows[number : number + 1]
 
 
 def shift(value, steps):
@@ -318,7 +391,7 @@
 
 
 def total_over(value):
-    for axis in ("sub", "dom"):
+    for axis in ("dom", "sub"):
         count = lax.axis_size(axis)
         if count & (count - 1):
             value = lax.psum(value, axis)
@@ -353,7 +426,7 @@
     subs = lax.axis_size("sub")
     halo = send_index.shape[2]
     blocks = 3 * subs
-    index = send_index.reshape(blocks, halo)
+    index = send_index.reshape(blocks, 1, halo)
     faces_total = faces * lax.axis_size("dom") * subs
     factor = 1.0 / math.sqrt(faces_total)
     wide = cells + blocks * halo
@@ -365,45 +438,85 @@
     across, up, down = exchange(outgoing)
     upper, lower = shift(up, -1), shift(down, 1)
     vectors = jnp.stack([edge_bias, edge_gain, edge_shift, node_bias, node_gain], axis=1)
-    local, ghost, edge_result, partial = pl.pallas_call(
+    senders, receivers = senders.reshape(1, faces), receivers.reshape(1, faces)
+    edge_first, node_first = edge_first.T, node_first.T
+    params = pltpu.CompilerParams(vmem_limit_bytes=48 * 1024 * 1024)
+    linear = pl.pallas_call(
+        functools.partial(early_kernel, tile=tile),
+        out_shape=shape((features, faces), F32),
+        compiler_params=params,
+        cost_estimate=pl.CostEstimate(flops=1 << 31, transcendentals=0, bytes_accessed=1 << 21),
+        name="early",
+    )(node_state, edge_state, senders, receivers, edge_first, vectors)
+    face_rows = shape((features, faces), BF16)
+    ghost, local, sender_sum, active, delta, hidden, node_partial = pl.pallas_call(
         functools.partial(main_kernel, tile=tile, factor=factor),
         out_shape=(
+            ghost_shape,
             shape((features, cells), F32),
-            ghost_shape,
-            shape((features, faces), BF16),
-            shape((4 * features, 2 * features), F32),
+            shape((wide // LOW * features, LOW), BF16),
+            face_rows,
+            face_rows,
+            face_rows,
+            shape((2 * features, 2 * features), F32),
         ),
         scratch_shapes=[
             pltpu.VMEM((wide // LOW * features, LOW), BF16),
             pltpu.VMEM((LOW, faces), BF16),
             pltpu.VMEM((LOW, faces), BF16),
             pltpu.VMEM((features, faces), F32),
-            pltpu.VMEM((features, faces), BF16),
             pltpu.VMEM((features, faces), F32),
             pltpu.VMEM((1, faces), F32),
         ],
-        compiler_params=pltpu.CompilerParams(vmem_limit_bytes=48 * 1024 * 1024),
+        compiler_params=params,
         name="main",
     )(
+        linear,
+        node_state,
+        across,
+        upper,
+        lower,
+        senders,
+        receivers,
+        node_cotangent,
+        edge_cotangent,
+        edge_first,
+        edge_second,
+        node_first,
+        node_second,
+        vectors,
+    )
+    partial, edge_result, local = pl.pallas_call(
+        functools.partial(late_kernel, tile=tile, factor=factor),
+        out_shape=(
+            shape((4 * features, 2 * features), F32),
+            face_rows,
+            shape((features, cells), F32),
+        ),
+        scratch_shapes=[pltpu.VMEM((wide // LOW * features, LOW), BF16)],
+        compiler_params=params,
+        cost_estimate=pl.CostEstimate(flops=1 << 31, transcendentals=0, bytes_accessed=1 << 21),
+        name="late",
+    )(
+        local,
+        sender_sum,
+        active,
+        delta,
+        hidden,
+        node_partial,
         node_state,
         across,
         upper,
         lower,
         edge_state,
-        senders.reshape(1, faces),
-        receivers.reshape(1, faces),
-        node_cotangent,
+        receivers,
         edge_cotangent,
-        edge_first.T,
-        edge_second,
-        node_first.T,
-        node_second,
-        vectors,
-    )
-    returned, forth, back = exchange(ghost)
-    further, nearer = shift(forth, 1), shift(back, -1)
+        edge_first,
+    )
+    shifted = (shift(ghost[:, 0], 1), ghost[:, 1], shift(ghost[:, 2], -1))
+    returned, further, nearer = exchange(jnp.stack(shifted, axis=1))
     totals = total_over(partial)
-    state, edgefirst, edgesecond, nodefirst, nodesecond, vector = pl.pallas_call(
+    state, edgefirst, edgesecond, nodefirst, nodesecond, *vector = pl.pallas_call(
         final_kernel,
         out_shape=(
             shape((features, cells), BF16),
@@ -411,10 +524,11 @@
             shape((features, features), F32),
             shape((features, 2 * features), F32),
             shape((features, features), F32),
-            shape((VECTORS, features), F32),
-        ),
+        )
+        + (shape((1, features), F32),) * VECTORS,
         name="final",
     )(local, returned, further, nearer, index, totals)
+    vector = [row.reshape(features) for row in vector]
     return (
         state,
         edge_result,

time: 72.9 us -> 64.4 us (0.88)
  blocking collectives: 9.68 us -> 0 us
  starting transfers between devices: 21.9 us -> 28.5 us
  local copies, waits for them, and re-layouts: 7.14 us -> 2.31 us
    all_to_all x1 -> x0, blocking collectives: 9.68 us -> none  [exchange(): lax.all_to_all(blocks, 'sub', split_axis=0, concat_axis=0, tiled=True)]
    all_to_all x1 -> x2, waiting for transfers between devices: 0.01 us -> 6.76 us  [exchange(): lax.all_to_all(blocks, 'sub', split_axis=0, concat_axis=0, tiled=True)]
    ppermute x5, waiting for transfers between devices: 11.9 us -> 5.49 us  [total_over(): lax.ppermute(value, axis, [(i, i ^ step) for i in range(count)])]
    unnamed x39 -> x34, local copies, waits for them, and re-layouts: 5.56 us -> 0.76 us
    all_to_all x1 -> x2, starting transfers between devices: 3.36 us -> 7.73 us  [exchange(): lax.all_to_all(blocks, 'sub', split_axis=0, concat_axis=0, tiled=True)]
    pallas_call x0 -> x2, Pallas kernels: none -> 4.1 us  [the longest x1 2.07 us: on_device(): pl.pallas_call(functools.partial(early_kernel, tile=tile), out_shape=shap...]
    pallas_call x1, Pallas kernels: 10.6 us -> 7.22 us  [on_device(): pl.pallas_call(functools.partial(main_kernel, tile=tile, factor=factor),...]
    ppermute x5, starting transfers between devices: 7.22 us -> 10.3 us  [total_over(): lax.ppermute(value, axis, [(i, i ^ step) for i in range(count)])]
  transfers between devices with their start and end apart: 10 -> 11, of which waited for: 7 -> 7; matrix products, arithmetic and copies ran while one was open for 1% -> 3% of each run, Pallas kernels for 0% -> 3%
where the time goes in v2:
time: 64.4 us; the launch traced here: 64 us
  starting transfers between devices  28.5 us (44%)
  waiting for transfers between devices  16 us (25%)
  Pallas kernels  15.5 us (24%)
  local copies, waits for them, and re-layouts  2.31 us (4%)
  between operations  0.91 us (1%)
  other arithmetic  0.75 us (1%)
    ppermute x4, starting transfers between devices, shift(): lax.ppermute(value, 'dom', [(source, source + steps) for source in range(...  10.5 us
    ppermute x5, starting transfers between devices, total_over(): lax.ppermute(value, axis, [(i, i ^ step) for i in range(count)])  10.3 us
    all_to_all x2, starting transfers between devices, exchange(): lax.all_to_all(blocks, 'sub', split_axis=0, concat_axis=0, tiled=True)  7.73 us
    pallas_call x1, Pallas kernels, on_device(): pl.pallas_call(functools.partial(main_kernel, tile=tile, factor=factor),...  7.22 us
    all_to_all x2, waiting for transfers between devices, exchange(): lax.all_to_all(blocks, 'sub', split_axis=0, concat_axis=0, tiled=True)  6.76 us
    ppermute x5, waiting for transfers between devices, total_over(): lax.ppermute(value, axis, [(i, i ^ step) for i in range(count)])  5.49 us
    ppermute x4, waiting for transfers between devices, shift(): lax.ppermute(value, 'dom', [(source, source + steps) for source in range(...  3.72 us
    pallas_call x1, Pallas kernels, on_device(): pl.pallas_call(final_kernel, out_shape=(shape((features, cells), BF16), s...  2.25 us
  transfers between devices with their start and end apart: 11, of which 7 were waited for; matrix products, arithmetic and copies ran while one was open for 3% of the time, Pallas kernels for 3%

profile of v2, /device:TPU:0, one launch (start us, length us, event | category | flops | bytes accessed | tf_op | source)
XLA Modules:
  0.0 64.0 jit_solution(97595748266732188)
XLA Ops:
  0.6 2.0 %pick.1 = bf16[4,3,64,128]{3,2,1,0:T(8,128)(2,1)} custom-call(bf16[64,1024]{1,0:T(8,128)(2,1)} %node_ref.7, s32[12,1,128]{2,1,0:T(1,128)} %bitcast.51), custom_call_target="tpu_custom_call" | custom-call | tf_op jit(solution)/shard_map/pick/pallas_call | solution.py:437
  2.6 4.4 %all-to-all-start = ((bf16[4,3,64,128]{3,2,1,0:T(8,128)(2,1)}), bf16[4,3,64,128]{3,2,1,0:T(8,128)(2,1)S(1)}, u32[]{:S(2)}, u32[]{:S(2)}) async-start(bf16[4,3,64,128]{3,2,1,0:T(8,128)(2,1)} %pick.1), calls=%async_computation | async-start | bytes 393216 | tf_op jit(solution)/shard_map/all_to_all | solution.py:389
  7.9 4.4 %all-to-all-done.across_ref = bf16[4,3,64,128]{3,2,1,0:T(8,128)(2,1)S(1)} async-done(((bf16[4,3,64,128]{3,2,1,0:T(8,128)(2,1)}), bf16[4,3,64,128]{3,2,1,0:T(8,128)(2,1)S(1)}, u32[]{:S(2)}, u32[]{:S(2)}) %all-to-all-start) | async-done | bytes 196640 | tf_op jit(solution)/shard_map/all_to_all | solution.py:389
  12.3 4.0 %collective-permute-start.1 = (bf16[4,64,128]{2,1,0:T(8,128)(2,1)S(1)}, bf16[4,64,128]{2,1,0:T(8,128)(2,1)S(1)}, u32[]{:S(2)}, u32[]{:S(2)}) collective-permute-start(bf16[4,64,128]{2,1,0:T(8,128)(2,1)S(1)} %get-tuple-element.58), channel_id=1, source_target_pairs={{0,4},{4,8},{8,12},{12,16},{16,20},{20,24},{24,28},{1,5},{5,9},{9,... | collective-permute-start | bytes 196616 | tf_op jit(solution)/shard_map/ppermute | solution.py:385
  16.3 1.3 %collective-permute-start = (bf16[4,64,128]{2,1,0:T(8,128)(2,1)S(1)}, bf16[4,64,128]{2,1,0:T(8,128)(2,1)S(1)}, u32[]{:S(2)}, u32[]{:S(2)}) collective-permute-start(bf16[4,64,128]{2,1,0:T(8,128)(2,1)S(1)} %get-tuple-element.59), channel_id=1, source_target_pairs={{4,0},{8,4},{12,8},{16,12},{20,16},{24,20},{28,24},{5,1},{9,5},{13... | collective-permute-start | bytes 196616 | tf_op jit(solution)/shard_map/ppermute | solution.py:385
  17.7 2.1 %early.1.linear_ref = f32[64,3072]{1,0:T(8,128)S(1)} custom-call(bf16[64,1024]{1,0:T(8,128)(2,1)S(1)} %copy-done, bf16[64,3072]{1,0:T(8,128)(2,1)S(1)} %copy-done.10, s32[1,3072]{1,0:T(1,128)S(1)} %bitcast.44, s32[1,3072]{1,0:T(1,128)S(1)} %bitcast.46, bf16[64,192]{1,0:T(8,128)(2,1)S(1)} %bitcast.40, f32[64,5]{1,0:T(8,128)S(1)} %copy.40.vectors_ref), custom_call_target="tpu_custom_call" | custom-call | flops 2147483648 | bytes 2097152 | tf_op jit(solution)/shard_map/early/pallas_call | solution.py:444
  19.8 2.7 %collective-permute-done.upper_ref = bf16[4,64,128]{2,1,0:T(8,128)(2,1)S(1)} collective-permute-done((bf16[4,64,128]{2,1,0:T(8,128)(2,1)S(1)}, bf16[4,64,128]{2,1,0:T(8,128)(2,1)S(1)}, u32[]{:S(2)}, u32[]{:S(2)}) %collective-permute-start) | collective-permute-done | bytes 65568 | tf_op jit(solution)/shard_map/ppermute | solution.py:385
  22.5 7.2 %main.1 = (bf16[4,3,64,128]{3,2,1,0:T(8,128)(2,1)S(1)}, f32[64,1024]{1,0:T(8,128)S(1)}, bf16[640,256]{1,0:T(8,128)(2,1)S(1)}, bf16[64,3072]{1,0:T(8,128)(2,1)S(1...) custom-call(f32[64,3072]{1,0:T(8,128)S(1)} %early.1.linear_ref, ...), custom_call_target="tpu_custom_call" | custom-call | tf_op jit(solution)/shard_map/main/pallas_call | solution.py:452
  29.7 2.0 %late.1 = (f32[256,128]{1,0:T(8,128)S(1)}, bf16[64,3072]{1,0:T(8,128)(2,1)}, f32[64,1024]{1,0:T(8,128)S(1)}) custom-call(f32[64,1024]{1,0:T(8,128)S(1)} %get-tuple-element.33.local_ref, bf16[640,256]{1,0:T(8,128)(2,1)S(1)} %get-tuple-element.34.sum_ref, bf16[64,3072]{1,0:T(8,128)(2,1)S(1)} %get-tuple-element.35.active_ref, ...), custom_call_target="tpu_custom_call" | custom-call | flops 2147483648 | bytes 2097152 | tf_op jit(solution)/shard_map/late/pallas_call | solution.py:489
  31.8 2.4 %collective-permute-start.4 = (f32[256,128]{1,0:T(8,128)S(1)}, f32[256,128]{1,0:T(8,128)S(1)}, u32[]{:S(2)}, u32[]{:S(2)}) collective-permute-start(f32[256,128]{1,0:T(8,128)S(1)} %get-tuple-element.41), channel_id=1, source_target_pairs={{0,4},{4,0},{8,12},{12,8},{16,20},{20,16},{24,28},{28,24},{1,5},{5... | collective-permute-start | bytes 393224 | tf_op jit(solution)/shard_map/ppermute | solution.py:401
  34.2 2.9 %collective-permute-done.4 = f32[256,128]{1,0:T(8,128)S(1)} collective-permute-done((f32[256,128]{1,0:T(8,128)S(1)}, f32[256,128]{1,0:T(8,128)S(1)}, u32[]{:S(2)}, u32[]{:S(2)}) %collective-permute-start.4) | collective-permute-done | bytes 131104 | tf_op jit(solution)/shard_map/ppermute | solution.py:401
  37.2 1.6 %collective-permute-start.5 = (f32[256,128]{1,0:T(8,128)S(1)}, f32[256,128]{1,0:T(8,128)S(1)}, u32[]{:S(2)}, u32[]{:S(2)}) collective-permute-start(f32[256,128]{1,0:T(8,128)S(1)} %add.15), channel_id=1, source_target_pairs={{0,8},{4,12},{8,0},{12,4},{16,24},{20,28},{24,16},{28,20},{1,9},{5... | collective-permute-start | bytes 393224 | tf_op jit(solution)/shard_map/ppermute | solution.py:401
  38.8 3.9 %collective-permute-start.2 = (bf16[4,64,128]{2,1,0:T(8,128)(2,1)S(1)}, bf16[4,64,128]{2,1,0:T(8,128)(2,1)S(1)}, u32[]{:S(2)}, u32[]{:S(2)}) collective-permute-start(bf16[4,64,128]{2,1,0:T(8,128)(2,1)S(1)} %get-tuple-element.56), channel_id=1, source_target_pairs={{0,4},{4,8},{8,12},{12,16},{16,20},{20,24},{24,28},{1,5},{5,9},{9,... | collective-permute-start | bytes 196616 | tf_op jit(solution)/shard_map/ppermute | solution.py:385
  42.7 1.3 %collective-permute-start.3 = (bf16[4,64,128]{2,1,0:T(8,128)(2,1)S(1)}, bf16[4,64,128]{2,1,0:T(8,128)(2,1)S(1)}, u32[]{:S(2)}, u32[]{:S(2)}) collective-permute-start(bf16[4,64,128]{2,1,0:T(8,128)(2,1)S(1)} %slice_bitcast_fusion.5), channel_id=1, source_target_pairs={{4,0},{8,4},{12,8},{16,12},{20,16},{24,20},{28,24},{5,1},{9,5},{13... | collective-permute-start | bytes 196616 | tf_op jit(solution)/shard_map/ppermute | solution.py:385
  44.1 3.8 %collective-permute-start.6 = (f32[256,128]{1,0:T(8,128)S(1)}, f32[256,128]{1,0:T(8,128)S(1)}, u32[]{:S(2)}, u32[]{:S(2)}) collective-permute-start(f32[256,128]{1,0:T(8,128)S(1)} %add.16), channel_id=1, source_target_pairs={{0,16},{4,20},{8,24},{12,28},{16,0},{20,4},{24,8},{28,12},{1,17},{... | collective-permute-start | bytes 393224 | tf_op jit(solution)/shard_map/ppermute | solution.py:401
  47.8 1.0 %collective-permute-done.3 = bf16[4,64,128]{2,1,0:T(8,128)(2,1)S(1)} collective-permute-done((bf16[4,64,128]{2,1,0:T(8,128)(2,1)S(1)}, bf16[4,64,128]{2,1,0:T(8,128)(2,1)S(1)}, u32[]{:S(2)}, u32[]{:S(2)}) %collective-permute-start.3) | collective-permute-done | bytes 65568 | tf_op jit(solution)/shard_map/ppermute | solution.py:385
  48.9 0.7 %copy.46 = bf16[4,3,64,128]{3,2,1,0:T(8,128)(2,1)} copy(bf16[4,3,64,128]{3,2,0,1:T(8,128)(2,1)S(1)} %pad_maximum_fusion) | data formatting | bytes 393216 | tf_op jit(solution)/shard_map/stack | solution.py:517
  49.6 3.4 %all-to-all-start.1 = ((bf16[4,3,64,128]{3,2,1,0:T(8,128)(2,1)}), bf16[4,3,64,128]{3,2,1,0:T(8,128)(2,1)S(1)}, u32[]{:S(2)}, u32[]{:S(2)}) async-start(bf16[4,3,64,128]{3,2,1,0:T(8,128)(2,1)} %copy.46), calls=%async_computation.1 | async-start | bytes 393216 | tf_op jit(solution)/shard_map/all_to_all | solution.py:389
  53.5 1.0 %collective-permute-done.7 = f32[256,128]{1,0:T(8,128)S(1)} collective-permute-done((f32[256,128]{1,0:T(8,128)S(1)}, f32[256,128]{1,0:T(8,128)S(1)}, u32[]{:S(2)}, u32[]{:S(2)}) %collective-permute-start.7) | collective-permute-done | bytes 131104 | tf_op jit(solution)/shard_map/ppermute | solution.py:401
  54.6 1.9 %collective-permute-start.8 = (f32[256,128]{1,0:T(8,128)S(1)}, f32[256,128]{1,0:T(8,128)S(1)}, u32[]{:S(2)}, u32[]{:S(2)}) collective-permute-start(f32[256,128]{1,0:T(8,128)S(1)} %add.18), channel_id=1, source_target_pairs={{0,2},{1,3},{2,0},{3,1},{4,6},{5,7},{6,4},{7,5},{8,10},{9,11},{10,... | collective-permute-start | bytes 393224 | tf_op jit(solution)/shard_map/ppermute | solution.py:401
  56.5 2.3 %all-to-all-done.1.across_ref = bf16[4,3,64,128]{3,2,1,0:T(8,128)(2,1)S(1)} async-done(((bf16[4,3,64,128]{3,2,1,0:T(8,128)(2,1)}), bf16[4,3,64,128]{3,2,1,0:T(8,128)(2,1)S(1)}, u32[]{:S(2)}, u32[]{:S(2)}) %all-to-all-start.1) | async-done | bytes 196640 | tf_op jit(solution)/shard_map/all_to_all | solution.py:389
  58.8 0.7 %slice_bitcast_fusion = (bf16[4,64,128]{2,1,0:T(8,128)(2,1)}, bf16[4,64,128]{2,1,0:T(8,128)(2,1)}) fusion(bf16[4,3,64,128]{3,2,1,0:T(8,128)(2,1)S(1)} %all-to-all-done.1.across_ref), kind=kLoop, calls=%fused_computation.1 | loop fusion | bytes 262144 | tf_op jit(solution)/shard_map/squeeze | solution.py:390
  59.5 1.5 %collective-permute-done.8 = f32[256,128]{1,0:T(8,128)S(1)} collective-permute-done((f32[256,128]{1,0:T(8,128)S(1)}, f32[256,128]{1,0:T(8,128)S(1)}, u32[]{:S(2)}, u32[]{:S(2)}) %collective-permute-start.8) | collective-permute-done | bytes 131104 | tf_op jit(solution)/shard_map/ppermute | solution.py:401
  61.7 2.2 %final.1 = (bf16[64,1024]{1,0:T(8,128)(2,1)}, f32[64,192]{1,0:T(8,128)}, f32[64,64]{1,0:T(8,128)}, f32[64,128]{1,0:T(8,128)}, f32[64,64]{1,0:T(8,128)}, /*index=...) custom-call(f32[64,1024]{1,0:T(8,128)} %copy-done.2, ...), custom_call_target="tpu_custom_call" | custom-call | tf_op jit(solution)/shard_map/final/pallas_call | solution.py:519
  (50 shorter events, 2.2 us)
Async XLA Ops:
  2.6 15.0 %copy-start.10 = (bf16[64,3072]{1,0:T(8,128)(2,1)S(1)}, bf16[64,3072]{1,0:T(8,128)(2,1)}, u32[]{:S(2)}) copy-start(bf16[64,3072]{1,0:T(8,128)(2,1)} %edge_ref.3) | copy-start | bytes 1179652
  2.6 9.7 %all-to-all-start = ((bf16[4,3,64,128]{3,2,1,0:T(8,128)(2,1)}), bf16[4,3,64,128]{3,2,1,0:T(8,128)(2,1)S(1)}, u32[]{:S(2)}, u32[]{:S(2)}) async-start(bf16[4,3,64,128]{3,2,1,0:T(8,128)(2,1)} %pick.1), calls=%async_computation | async-start | bytes 393216 | tf_op jit(solution)/shard_map/all_to_all | solution.py:389
  7.0 0.7 %copy-start.14 = (f32[64]{0:T(128)S(1)}, f32[64]{0:T(128)}, u32[]{:S(2)}) copy-start(f32[64]{0:T(128)} %param.27) | copy-start | bytes 772
  7.8 9.8 %copy-start = (bf16[64,1024]{1,0:T(8,128)(2,1)S(1)}, bf16[64,1024]{1,0:T(8,128)(2,1)}, u32[]{:S(2)}) copy-start(bf16[64,1024]{1,0:T(8,128)(2,1)} %node_ref.7) | copy-start | bytes 393220
  7.8 9.8 %copy-start.4 = (bf16[192,64]{0,1:T(8,128)(2,1)S(1)}, bf16[192,64]{0,1:T(8,128)(2,1)}, u32[]{:S(2)}) copy-start(bf16[192,64]{0,1:T(8,128)(2,1)} %param.23) | copy-start | bytes 73732
  7.8 9.8 %copy-start.8 = (s32[3072]{0:T(1024)S(1)}, s32[3072]{0:T(1024)}, u32[]{:S(2)}) copy-start(s32[3072]{0:T(1024)} %param.18) | copy-start | bytes 36868
  7.8 9.8 %copy-start.9 = (s32[3072]{0:T(1024)S(1)}, s32[3072]{0:T(1024)}, u32[]{:S(2)}) copy-start(s32[3072]{0:T(1024)} %param.19) | copy-start | bytes 36868
  12.3 7.5 %collective-permute-start.1 = (bf16[4,64,128]{2,1,0:T(8,128)(2,1)S(1)}, bf16[4,64,128]{2,1,0:T(8,128)(2,1)S(1)}, u32[]{:S(2)}, u32[]{:S(2)}) collective-permute-start(bf16[4,64,128]{2,1,0:T(8,128)(2,1)S(1)} %get-tuple-element.58), channel_id=1, source_target_pairs={{0,4},{4,8},{8,12},{12,16},{16,20},{20,24},{24,28},{1,5},{5,9},{9,... | collective-permute-start | bytes 196616 | tf_op jit(solution)/shard_map/ppermute | solution.py:385
  16.3 6.2 %collective-permute-start = (bf16[4,64,128]{2,1,0:T(8,128)(2,1)S(1)}, bf16[4,64,128]{2,1,0:T(8,128)(2,1)S(1)}, u32[]{:S(2)}, u32[]{:S(2)}) collective-permute-start(bf16[4,64,128]{2,1,0:T(8,128)(2,1)S(1)} %get-tuple-element.59), channel_id=1, source_target_pairs={{4,0},{8,4},{12,8},{16,12},{20,16},{24,20},{28,24},{5,1},{9,5},{13... | collective-permute-start | bytes 196616 | tf_op jit(solution)/shard_map/ppermute | solution.py:385
  17.7 4.8 %copy-start.1 = (bf16[64,3072]{1,0:T(8,128)(2,1)S(1)}, bf16[64,3072]{1,0:T(8,128)(2,1)}, u32[]{:S(2)}) copy-start(bf16[64,3072]{1,0:T(8,128)(2,1)} %edgecot_ref.3) | copy-start | bytes 1179652
  17.7 4.8 %copy-start.3 = (bf16[64,1024]{1,0:T(8,128)(2,1)S(1)}, bf16[64,1024]{1,0:T(8,128)(2,1)}, u32[]{:S(2)}) copy-start(bf16[64,1024]{1,0:T(8,128)(2,1)} %nodecot_ref.1) | copy-start | bytes 393220
  17.7 4.8 %copy-start.5 = (bf16[64,64]{1,0:T(8,128)(2,1)S(1)}, bf16[64,64]{1,0:T(8,128)(2,1)}, u32[]{:S(2)}) copy-start(bf16[64,64]{1,0:T(8,128)(2,1)} %edgesecond_ref.1) | copy-start | bytes 24580
  17.7 4.8 %copy-start.6 = (bf16[128,64]{0,1:T(8,128)(2,1)S(1)}, bf16[128,64]{0,1:T(8,128)(2,1)}, u32[]{:S(2)}) copy-start(bf16[128,64]{0,1:T(8,128)(2,1)} %param.28) | copy-start | bytes 49156
  17.7 4.8 %copy-start.7 = (bf16[64,64]{1,0:T(8,128)(2,1)S(1)}, bf16[64,64]{1,0:T(8,128)(2,1)}, u32[]{:S(2)}) copy-start(bf16[64,64]{1,0:T(8,128)(2,1)} %nodesecond_ref.1) | copy-start | bytes 24580
  31.8 5.4 %copy-start.2 = (f32[64,1024]{1,0:T(8,128)}, f32[64,1024]{1,0:T(8,128)S(1)}, u32[]{:S(2)}) copy-start(f32[64,1024]{1,0:T(8,128)S(1)} %get-tuple-element.39.local_ref) | copy-start | bytes 786436
  31.8 5.4 %collective-permute-start.4 = (f32[256,128]{1,0:T(8,128)S(1)}, f32[256,128]{1,0:T(8,128)S(1)}, u32[]{:S(2)}, u32[]{:S(2)}) collective-permute-start(f32[256,128]{1,0:T(8,128)S(1)} %get-tuple-element.41), channel_id=1, source_target_pairs={{0,4},{4,0},{8,12},{12,8},{16,20},{20,16},{24,28},{28,24},{1,5},{5... | collective-permute-start | bytes 393224 | tf_op jit(solution)/shard_map/ppermute | solution.py:401
  37.2 6.9 %collective-permute-start.5 = (f32[256,128]{1,0:T(8,128)S(1)}, f32[256,128]{1,0:T(8,128)S(1)}, u32[]{:S(2)}, u32[]{:S(2)}) collective-permute-start(f32[256,128]{1,0:T(8,128)S(1)} %add.15), channel_id=1, source_target_pairs={{0,8},{4,12},{8,0},{12,4},{16,24},{20,28},{24,16},{28,20},{1,9},{5... | collective-permute-start | bytes 393224 | tf_op jit(solution)/shard_map/ppermute | solution.py:401
  38.8 9.0 %collective-permute-start.2 = (bf16[4,64,128]{2,1,0:T(8,128)(2,1)S(1)}, bf16[4,64,128]{2,1,0:T(8,128)(2,1)S(1)}, u32[]{:S(2)}, u32[]{:S(2)}) collective-permute-start(bf16[4,64,128]{2,1,0:T(8,128)(2,1)S(1)} %get-tuple-element.56), channel_id=1, source_target_pairs={{0,4},{4,8},{8,12},{12,16},{16,20},{20,24},{24,28},{1,5},{5,9},{9,... | collective-permute-start | bytes 196616 | tf_op jit(solution)/shard_map/ppermute | solution.py:385
  42.7 6.2 %collective-permute-start.3 = (bf16[4,64,128]{2,1,0:T(8,128)(2,1)S(1)}, bf16[4,64,128]{2,1,0:T(8,128)(2,1)S(1)}, u32[]{:S(2)}, u32[]{:S(2)}) collective-permute-start(bf16[4,64,128]{2,1,0:T(8,128)(2,1)S(1)} %slice_bitcast_fusion.5), channel_id=1, source_target_pairs={{4,0},{8,4},{12,8},{16,12},{20,16},{24,20},{28,24},{5,1},{9,5},{13... | collective-permute-start | bytes 196616 | tf_op jit(solution)/shard_map/ppermute | solution.py:385
  44.1 8.9 %collective-permute-start.6 = (f32[256,128]{1,0:T(8,128)S(1)}, f32[256,128]{1,0:T(8,128)S(1)}, u32[]{:S(2)}, u32[]{:S(2)}) collective-permute-start(f32[256,128]{1,0:T(8,128)S(1)} %add.16), channel_id=1, source_target_pairs={{0,16},{4,20},{8,24},{12,28},{16,0},{20,4},{24,8},{28,12},{1,17},{... | collective-permute-start | bytes 393224 | tf_op jit(solution)/shard_map/ppermute | solution.py:401
  49.6 9.2 %all-to-all-start.1 = ((bf16[4,3,64,128]{3,2,1,0:T(8,128)(2,1)}), bf16[4,3,64,128]{3,2,1,0:T(8,128)(2,1)S(1)}, u32[]{:S(2)}, u32[]{:S(2)}) async-start(bf16[4,3,64,128]{3,2,1,0:T(8,128)(2,1)} %copy.46), calls=%async_computation.1 | async-start | bytes 393216 | tf_op jit(solution)/shard_map/all_to_all | solution.py:389
  53.0 1.6 %collective-permute-start.7 = (f32[256,128]{1,0:T(8,128)S(1)}, f32[256,128]{1,0:T(8,128)S(1)}, u32[]{:S(2)}, u32[]{:S(2)}) collective-permute-start(f32[256,128]{1,0:T(8,128)S(1)} %add.17), channel_id=1, source_target_pairs={{0,1},{1,0},{2,3},{3,2},{4,5},{5,4},{6,7},{7,6},{8,9},{9,8},{10,11... | collective-permute-start | bytes 393224 | tf_op jit(solution)/shard_map/ppermute | solution.py:401
  54.6 6.5 %collective-permute-start.8 = (f32[256,128]{1,0:T(8,128)S(1)}, f32[256,128]{1,0:T(8,128)S(1)}, u32[]{:S(2)}, u32[]{:S(2)}) collective-permute-start(f32[256,128]{1,0:T(8,128)S(1)} %add.18), channel_id=1, source_target_pairs={{0,2},{1,3},{2,0},{3,1},{4,6},{5,7},{6,4},{7,5},{8,10},{9,11},{10,... | collective-permute-start | bytes 393224 | tf_op jit(solution)/shard_map/ppermute | solution.py:401
  58.8 2.9 %copy-start.11 = (bf16[4,3,64,128]{3,2,1,0:T(8,128)(2,1)}, bf16[4,3,64,128]{3,2,1,0:T(8,128)(2,1)S(1)}, u32[]{:S(2)}) copy-start(bf16[4,3,64,128]{3,2,1,0:T(8,128)(2,1)S(1)} %all-to-all-done.1.across_ref) | copy-start | bytes 589828
  (4 other events, 2.7 us)
